TPU v7x, 128 devices: a whole 4x4x4 slice. The times are simulated.
128 devices in a mesh: ctx: 16 (over y, x), ch: 8 (over z, core).
Axes of the slice: x: 4, y: 4, z: 4, core: 2. Of those that a mesh axis runs over, the one named last changes fastest.
Arguments:
- projected: bfloat16 [3, 16384, 1024], P(None, 'ctx', 'ch'), may hold values from -6 to 6
- short_taps: float32 [3, 3, 1024], P(None, None, 'ch'), may hold values from -3 to 3
- long_filter: float32 [16384, 1024], P('ctx', 'ch'), may hold values from -1 to 1
- grad_mixed: bfloat16 [16384, 1024], P('ctx', 'ch'), may hold values from -6 to 6
Outputs:
- mixed: bfloat16 [16384, 1024], P('ctx', 'ch')
- grad_streams: bfloat16 [3, 16384, 1024], P(None, 'ctx', 'ch')
- grad_filter: float32 [16384, 1024], P('ctx', 'ch')
All inputs are finite; a program needn't handle non-finite values.
Results may differ from a plain program's by a relative error of at most 0.0011.
Values may be sent and summed in bfloat16 or wider, within the bound.
A program may use at most 128 MiB of HBM per device.

v0:
```python
import math

import jax
import jax.numpy as jnp
from jax import lax
from jax.sharding import PartitionSpec as P


def passed_along(value, axis, steps):
    count = lax.axis_size(axis)
    first, last = (max(0, -steps), min(count, count - steps))
    return lax.ppermute(value, axis, [(source, source + steps) for source in range(first, last)])


def cos_sin(numer, denom):
    angle = 2.0 * math.pi / denom * numer.astype(jnp.float32)
    return (jnp.cos(angle), jnp.sin(angle))


def dft_table(points, sign):
    index_all = jnp.arange(points, dtype=jnp.int32)
    wrapped = index_all[:, None] * index_all[None, :] % points
    cosine, sine_part = cos_sin(wrapped, points)
    return (cosine, sign * sine_part)


def mixing(table_part, values_in, along_axis):
    return jnp.tensordot(
        table_part, values_in, axes=((0,), (along_axis,)), precision=lax.Precision.HIGHEST
    )


def contract_axis(real_part, imag_part, table_pair, along_axis):
    cosine, sine_part = table_pair
    out_real = mixing(cosine, real_part, along_axis) - mixing(sine_part, imag_part, along_axis)
    out_imag = mixing(sine_part, real_part, along_axis) + mixing(cosine, imag_part, along_axis)
    return (out_real, out_imag)


def contract_real(real_part, table_pair):
    cosine, sine_part = table_pair
    return (mixing(cosine, real_part, 0), mixing(sine_part, real_part, 0))


def rotate(real_part, imag_part, cosine, sine_part):
    return (real_part * cosine - imag_part * sine_part, real_part * sine_part + imag_part * cosine)


def local_dft(real_part, imag_part, sign):
    count_len = real_part.shape[0]
    first_len = 1
    for factor in range(1, math.isqrt(count_len) + 1):
        if count_len % factor == 0:
            first_len = factor
    second = count_len // first_len
    trailing = real_part.shape[1:]
    real_part = real_part.reshape((first_len, second) + trailing)
    imag_part = imag_part.reshape((first_len, second) + trailing)
    real_part, imag_part = contract_axis(real_part, imag_part, dft_table(first_len, sign), 0)
    index_one = jnp.arange(first_len, dtype=jnp.int32)[:, None]
    index_two = jnp.arange(second, dtype=jnp.int32)[None, :]
    cosine, sine_part = cos_sin(index_one * index_two % count_len, count_len)
    expand = (first_len, second) + (1,) * len(trailing)
    real_part, imag_part = rotate(
        real_part, imag_part, cosine.reshape(expand), sign * sine_part.reshape(expand)
    )
    real_part, imag_part = contract_axis(real_part, imag_part, dft_table(second, sign), 1)
    return (real_part.reshape((count_len,) + trailing), imag_part.reshape((count_len,) + trailing))


def spread_forward(received, devices, block_rows, total_len, own_index):
    piece_rows = received.shape[0] // devices
    shaped = received.reshape((devices, piece_rows) + received.shape[1:])
    offset = own_index * piece_rows + jnp.arange(piece_rows, dtype=jnp.int32)
    source = jnp.arange(devices, dtype=jnp.int32)
    position = source[:, None] * block_rows + offset[None, :]
    cosine, sine_part = cos_sin(position % (2 * total_len), 2 * total_len)
    cosine = cosine[:, :, None, None]
    sine_part = sine_part[:, :, None, None]
    table_pair = dft_table(devices, -1.0)
    even_real, even_imag = contract_real(shaped, table_pair)
    odd_real, odd_imag = contract_axis(shaped * cosine, -(shaped * sine_part), table_pair, 0)
    real_part = jnp.stack([even_real, odd_real], axis=2)
    imag_part = jnp.stack([even_imag, odd_imag], axis=2)
    turn_cos, turn_sin = cos_sin(source[:, None] * offset[None, :] % total_len, total_len)
    turn_cos = turn_cos[:, :, None, None, None]
    turn_sin = turn_sin[:, :, None, None, None]
    real_part, imag_part = rotate(real_part, imag_part, turn_cos, -turn_sin)
    full_shape = (devices * piece_rows,) + real_part.shape[2:]
    return (real_part.reshape(full_shape), imag_part.reshape(full_shape))


def spectral_products(real_part, imag_part):
    filter_real, filter_imag = (real_part[:, :, 0], imag_part[:, :, 0])
    value_real, value_imag = (real_part[:, :, 1], imag_part[:, :, 1])
    back_real, back_imag = (real_part[:, :, 2], imag_part[:, :, 2])
    conv_real = filter_real * value_real - filter_imag * value_imag
    conv_imag = filter_real * value_imag + filter_imag * value_real
    stream_real = filter_real * back_real + filter_imag * back_imag
    stream_imag = filter_real * back_imag - filter_imag * back_real
    filt_real = value_real * back_real + value_imag * back_imag
    filt_imag = value_real * back_imag - value_imag * back_real
    return (
        jnp.stack([conv_real, stream_real, filt_real], axis=2),
        jnp.stack([conv_imag, stream_imag, filt_imag], axis=2),
    )


def spectral_middle(real_part, imag_part, own_index, total_len):
    real_part, imag_part = local_dft(real_part, imag_part, -1.0)
    real_part, imag_part = spectral_products(real_part, imag_part)
    real_part, imag_part = local_dft(real_part, imag_part, 1.0)
    count_len = real_part.shape[0]
    cosine, sine_part = cos_sin(
        jnp.arange(count_len, dtype=jnp.int32) * own_index % total_len, total_len
    )
    return rotate(real_part, imag_part, cosine[:, None, None, None], sine_part[:, None, None, None])


def spread_inverse(received, devices, block_rows, total_len, own_index):
    real_part, imag_part = received
    piece_rows = real_part.shape[0] // devices
    full_shape = (devices, piece_rows) + real_part.shape[1:]
    real_part, imag_part = contract_axis(
        real_part.reshape(full_shape), imag_part.reshape(full_shape), dft_table(devices, 1.0), 0
    )
    offset = own_index * piece_rows + jnp.arange(piece_rows, dtype=jnp.int32)
    source = jnp.arange(devices, dtype=jnp.int32)
    position = source[:, None] * block_rows + offset[None, :]
    cosine, sine_part = cos_sin(position % (2 * total_len), 2 * total_len)
    cosine = cosine[:, :, None, None]
    sine_part = sine_part[:, :, None, None]
    merged = (real_part[:, :, 0] + real_part[:, :, 1] * cosine - imag_part[:, :, 1] * sine_part) * (
        0.5 / total_len
    )
    return merged.reshape((devices * piece_rows,) + merged.shape[2:])


def along_context(signals, total_len):
    devices = lax.axis_size("ctx")
    own_index = lax.axis_index("ctx")
    block_rows = signals.shape[0]
    real_part, imag_part = spread_forward(
        lax.all_to_all(signals, "ctx", split_axis=0, concat_axis=0, tiled=True),
        devices,
        block_rows,
        total_len,
        own_index,
    )
    real_part, imag_part = (
        lax.all_to_all(real_part, "ctx", split_axis=0, concat_axis=0, tiled=True),
        lax.all_to_all(imag_part, "ctx", split_axis=0, concat_axis=0, tiled=True),
    )
    real_part, imag_part = spectral_middle(real_part, imag_part, own_index, total_len)
    merged = spread_inverse(
        (
            lax.all_to_all(real_part, "ctx", split_axis=0, concat_axis=0, tiled=True),
            lax.all_to_all(imag_part, "ctx", split_axis=0, concat_axis=0, tiled=True),
        ),
        devices,
        block_rows,
        total_len,
        own_index,
    )
    return lax.all_to_all(merged, "ctx", split_axis=0, concat_axis=0, tiled=True)


def local(projected, short_taps, long_filter, grad_mixed):
    tok_rows = projected.shape[1]
    prev_rows = passed_along(projected[:, tok_rows - 2 :, :], "ctx", 1)
    extended = jnp.concatenate([prev_rows, projected], axis=1).astype(jnp.float32)
    streams = (
        short_taps[:, 0][:, None, :] * extended[:, 2:]
        + short_taps[:, 1][:, None, :] * extended[:, 1 : tok_rows + 1]
        + short_taps[:, 2][:, None, :] * extended[:, 0:tok_rows]
    )
    query_stream, key_stream, value_stream = (streams[0], streams[1], streams[2])
    key_value = key_stream * value_stream
    grad_float = grad_mixed.astype(jnp.float32)
    back_gated = grad_float * query_stream
    signals = jnp.stack([long_filter, key_value, back_gated], axis=1)
    total_len = tok_rows * lax.axis_size("ctx")
    results = along_context(signals, total_len)
    conv_out, corr_stream, corr_filt = (results[:, 0], results[:, 1], results[:, 2])
    mixed = (query_stream * conv_out).astype(jnp.bfloat16)
    grad_streams = jnp.stack(
        [grad_float * conv_out, corr_stream * value_stream, corr_stream * key_stream]
    ).astype(jnp.bfloat16)
    grad_filter = corr_filt * (1.0 / math.sqrt(total_len))
    return (mixed, grad_streams, grad_filter)


def solution(mesh):
    in_specs = (P(None, "ctx", "ch"), P(None, None, "ch"), P("ctx", "ch"), P("ctx", "ch"))
    out_specs = (P("ctx", "ch"), P(None, "ctx", "ch"), P("ctx", "ch"))
    return jax.shard_map(local, mesh=mesh, in_specs=in_specs, out_specs=out_specs, check_vma=False)
```

profile of v0, /device:TPU:0, one launch (start us, length us, event | category | flops | bytes accessed | tf_op | source)
XLA Modules:
  0.0 406.2 jit_solution(6521692518379682959)
XLA Ops:
  11.2 8.4 %all-to-all-start = ((f32[1024,3,128]{2,1,0:T(4,128)}), f32[1024,3,128]{2,1,0:T(4,128)}, u32[]{:S(2)}, u32[]{:S(2)}) async-start(f32[1024,3,128]{2,1,0:T(4,128)} %pad_maximum_fusion.2), calls=%async_computation | async-start | bytes 4194304 | tf_op jit(solution)/shard_map/all_to_all | solution.py:144
  20.1 28.4 %all-to-all-done = f32[1024,3,128]{2,1,0:T(4,128)} async-done(((f32[1024,3,128]{2,1,0:T(4,128)}), f32[1024,3,128]{2,1,0:T(4,128)}, u32[]{:S(2)}, u32[]{:S(2)}) %all-to-all-start) | async-done | bytes 1572896 | tf_op jit(solution)/shard_map/all_to_all | solution.py:144
  68.9 4.1 %copy.121 = f32[1024,2,3,128]{3,1,2,0:T(2,128)} copy(f32[1024,2,3,128]{3,0,2,1:T(8,128)S(1)} %get-tuple-element.10) | data formatting | bytes 6291456 | tf_op jit(solution)/shard_map/add | solution.py:46
  73.0 4.5 %all-to-all-start.2 = ((f32[1024,2,3,128]{3,1,2,0:T(2,128)}), f32[1024,2,3,128]{3,1,2,0:T(2,128)}, u32[]{:S(2)}, u32[]{:S(2)}) async-start(f32[1024,2,3,128]{3,1,2,0:T(2,128)} %copy.121), calls=%async_computation.2 | async-start | bytes 6291456 | tf_op jit(solution)/shard_map/all_to_all | solution.py:152
  77.5 6.0 %copy.118 = f32[1024,2,3,128]{3,1,2,0:T(2,128)} copy(f32[1024,2,3,128]{3,0,2,1:T(8,128)} %get-tuple-element.9) | data formatting | bytes 6291456 | tf_op jit(solution)/shard_map/sub | solution.py:46
  83.5 37.6 %all-to-all-done.2 = f32[1024,2,3,128]{3,1,2,0:T(2,128)} async-done(((f32[1024,2,3,128]{3,1,2,0:T(2,128)}), f32[1024,2,3,128]{3,1,2,0:T(2,128)}, u32[]{:S(2)}, u32[]{:S(2)}) %all-to-all-start.2) | async-done | bytes 3145760 | tf_op jit(solution)/shard_map/all_to_all | solution.py:152
  121.1 4.7 %all-to-all-start.1 = ((f32[1024,2,3,128]{3,1,2,0:T(2,128)}), f32[1024,2,3,128]{3,1,2,0:T(2,128)}, u32[]{:S(2)}, u32[]{:S(2)}) async-start(f32[1024,2,3,128]{3,1,2,0:T(2,128)} %copy.118), calls=%async_computation.1 | async-start | bytes 6291456 | tf_op jit(solution)/shard_map/all_to_all | solution.py:151
  128.1 6.9 %fusion.28 = f32[32,32,2,3,128]{4,0,3,2,1:T(8,128)} fusion(f32[32,32,2,3,128]{4,1,0,3,2:T(8,128)S(1)} %bitcast.149), kind=kOutput, calls=%fused_computation.40 | convolution fusion | flops 302005248 | bytes 6291456 | tf_op jit(solution)/shard_map/dot_general | solution.py:28
  135.0 6.8 %fusion.26 = f32[32,32,2,3,128]{4,0,3,2,1:T(8,128)} fusion(f32[32,32,2,3,128]{4,1,0,3,2:T(8,128)S(1)} %bitcast.150), kind=kOutput, calls=%fused_computation.38 | convolution fusion | flops 302004224 | bytes 6291456 | tf_op jit(solution)/shard_map/dot_general | solution.py:28
  141.8 26.5 %all-to-all-done.1 = f32[1024,2,3,128]{3,1,2,0:T(2,128)} async-done(((f32[1024,2,3,128]{3,1,2,0:T(2,128)}), f32[1024,2,3,128]{3,1,2,0:T(2,128)}, u32[]{:S(2)}, u32[]{:S(2)}) %all-to-all-start.1) | async-done | bytes 3145760 | tf_op jit(solution)/shard_map/all_to_all | solution.py:151
  171.1 5.8 %fusion.34 = f32[32,32,2,3,128]{4,0,3,2,1:T(8,128)S(1)} fusion(f32[32,32,2,3,128]{4,0,3,2,1:T(8,128)S(1)} %copy-done.1, f32[32,32,2,3,128]{4,1,0,3,2:T(8,128)S(1)} %bitcast.155), kind=kOutput, calls=%fused_computation.47 | convolution fusion | flops 302790656 | bytes 9437184 | tf_op jit(solution)/shard_map/dot_general | solution.py:28
  176.9 6.1 %multiply_subtract_fusion.1 = (f32[32,32,2,3,128]{4,0,3,2,1:T(8,128)S(1)}, f32[32,32,2,3,128]{4,0,3,2,1:T(8,128)S(1)}) fusion(f32[32,32,2,3,128]{4,0,3,2,1:T(8,128)S(1)} %fusion.34, f32[32,32]{0,1:T(8,128)S(1)} %get-tuple-element.43, f32[32,32]{0,1:T(8,128)S(1)} %get-tuple-element.44, f32[32,32,2,3,128]{4,0,3,2,1:T(8,128)S(1)} %copy-done.2, ...), kind=kOutput, calls=%fused_computation.11 | convolution fusion | flops 307510272 | bytes 15736832 | tf_op jit(solution)/shard_map/dot_general | solution.py:28
  183.0 5.4 %fusion.20 = f32[32,32,2,3,128]{4,0,3,2,1:T(8,128)S(1)} fusion(f32[32,32,2,3,128]{4,0,3,2,1:T(8,128)S(1)} %get-tuple-element.6), kind=kOutput, calls=%fused_computation.32 | convolution fusion | flops 302005248 | bytes 6291456 | tf_op jit(solution)/shard_map/dot_general | solution.py:28
  188.4 5.3 %fusion.18 = f32[32,32,2,3,128]{4,0,3,2,1:T(8,128)S(1)} fusion(f32[32,32,2,3,128]{4,0,3,2,1:T(8,128)S(1)} %get-tuple-element.6), kind=kOutput, calls=%fused_computation.30 | convolution fusion | flops 302004224 | bytes 6291456 | tf_op jit(solution)/shard_map/dot_general | solution.py:28
  193.7 5.6 %fusion.40 = f32[32,32,2,3,128]{4,0,3,2,1:T(8,128)S(1)} fusion(f32[32,32,2,3,128]{4,0,3,2,1:T(8,128)S(1)} %fusion.20, f32[32,32,2,3,128]{4,0,3,2,1:T(8,128)S(1)} %get-tuple-element.5), kind=kOutput, calls=%fused_computation.49 | convolution fusion | flops 302790656 | bytes 9437184 | tf_op jit(solution)/shard_map/dot_general | solution.py:28
  201.1 5.3 %fusion.43 = f32[32,32,2,3,128]{4,0,3,2,1:T(8,128)S(1)} fusion(f32[32,32,2,3,128]{4,0,3,2,1:T(8,128)S(1)} %fusion.18, f32[32,32,2,3,128]{4,0,3,2,1:T(8,128)S(1)} %get-tuple-element.5), kind=kOutput, calls=%fused_computation.50 | convolution fusion | flops 302791680 | bytes 9437184 | tf_op jit(solution)/shard_map/dot_general | solution.py:28
  222.2 3.8 multiply_subtract_fusion
  226.0 5.3 %fusion.12 = f32[32,32,2,3,128]{4,0,3,2,1:T(8,128)S(1)} fusion(f32[32,32,2,3,128]{4,0,3,2,1:T(8,128)S(1)} %get-tuple-element.4), kind=kOutput, calls=%fused_computation.24 | convolution fusion | flops 302004224 | bytes 6291456 | tf_op jit(solution)/shard_map/dot_general | solution.py:28
  231.3 5.5 %fusion.10 = f32[32,32,2,3,128]{4,0,3,2,1:T(8,128)S(1)} fusion(f32[32,32,2,3,128]{4,0,3,2,1:T(8,128)S(1)} %get-tuple-element.4), kind=kOutput, calls=%fused_computation.22 | convolution fusion | flops 302004224 | bytes 6291456 | tf_op jit(solution)/shard_map/dot_general | solution.py:28
  236.8 5.3 %fusion.46 = f32[32,32,2,3,128]{4,0,3,2,1:T(8,128)S(1)} fusion(f32[32,32,2,3,128]{4,0,3,2,1:T(8,128)S(1)} %fusion.12, f32[32,32,2,3,128]{4,0,3,2,1:T(8,128)S(1)} %get-tuple-element.3), kind=kOutput, calls=%fused_computation.51 | convolution fusion | flops 302790656 | bytes 9437184 | tf_op jit(solution)/shard_map/dot_general | solution.py:28
  243.9 5.7 %fusion.49 = f32[32,32,2,3,128]{4,0,3,2,1:T(8,128)S(1)} fusion(f32[32,32,2,3,128]{4,0,3,2,1:T(8,128)S(1)} %fusion.10, f32[32,32,2,3,128]{4,0,3,2,1:T(8,128)S(1)} %get-tuple-element.3), kind=kOutput, calls=%fused_computation.52 | convolution fusion | flops 302790656 | bytes 9437184 | tf_op jit(solution)/shard_map/dot_general | solution.py:28
  253.9 4.1 %copy.147 = f32[1024,2,3,128]{3,1,2,0:T(2,128)} copy(f32[1024,2,3,128]{3,0,2,1:T(8,128)S(1)} %get-tuple-element.8) | data formatting | bytes 6291456 | tf_op jit(solution)/shard_map/add | solution.py:46
  258.0 4.5 %all-to-all-start.4 = ((f32[1024,2,3,128]{3,1,2,0:T(2,128)}), f32[1024,2,3,128]{3,1,2,0:T(2,128)}, u32[]{:S(2)}, u32[]{:S(2)}) async-start(f32[1024,2,3,128]{3,1,2,0:T(2,128)} %copy.147), calls=%async_computation.4 | async-start | bytes 6291456 | tf_op jit(solution)/shard_map/all_to_all | solution.py:158
  262.5 6.0 %copy.144 = f32[1024,2,3,128]{3,1,2,0:T(2,128)} copy(f32[1024,2,3,128]{3,0,2,1:T(8,128)} %get-tuple-element.7) | data formatting | bytes 6291456 | tf_op jit(solution)/shard_map/sub | solution.py:46
  268.4 37.5 %all-to-all-done.4 = f32[1024,2,3,128]{3,1,2,0:T(2,128)} async-done(((f32[1024,2,3,128]{3,1,2,0:T(2,128)}), f32[1024,2,3,128]{3,1,2,0:T(2,128)}, u32[]{:S(2)}, u32[]{:S(2)}) %all-to-all-start.4) | async-done | bytes 3145760 | tf_op jit(solution)/shard_map/all_to_all | solution.py:158
  306.0 4.7 %all-to-all-start.3 = ((f32[1024,2,3,128]{3,1,2,0:T(2,128)}), f32[1024,2,3,128]{3,1,2,0:T(2,128)}, u32[]{:S(2)}, u32[]{:S(2)}) async-start(f32[1024,2,3,128]{3,1,2,0:T(2,128)} %copy.144), calls=%async_computation.3 | async-start | bytes 6291456 | tf_op jit(solution)/shard_map/all_to_all | solution.py:157
  312.7 6.7 %fusion.4 = f32[16,64,2,3,128]{4,0,3,2,1:T(8,128)} fusion(f32[16,64,2,3,128]{4,1,0,3,2:T(8,128)S(1)} %bitcast.151), kind=kOutput, calls=%fused_computation.16 | convolution fusion | flops 150998528 | bytes 6291456 | tf_op jit(solution)/shard_map/dot_general | solution.py:28
  319.4 6.7 %fusion.2 = f32[16,64,2,3,128]{4,0,3,2,1:T(8,128)} fusion(f32[16,64,2,3,128]{4,1,0,3,2:T(8,128)S(1)} %bitcast.152), kind=kOutput, calls=%fused_computation.14 | convolution fusion | flops 150998528 | bytes 6291456 | tf_op jit(solution)/shard_map/dot_general | solution.py:28
  326.1 27.2 %all-to-all-done.3 = f32[1024,2,3,128]{3,1,2,0:T(2,128)} async-done(((f32[1024,2,3,128]{3,1,2,0:T(2,128)}), f32[1024,2,3,128]{3,1,2,0:T(2,128)}, u32[]{:S(2)}, u32[]{:S(2)}) %all-to-all-start.3) | async-done | bytes 3145760 | tf_op jit(solution)/shard_map/all_to_all | solution.py:157
  355.4 5.3 %fusion.6 = f32[16,64,2,3,128]{4,0,3,2,1:T(8,128)S(1)} fusion(f32[16,64,2,3,128]{4,1,0,3,2:T(8,128)S(1)} %bitcast.153), kind=kOutput, calls=%fused_computation.18 | convolution fusion | flops 150998528 | bytes 6291456 | tf_op jit(solution)/shard_map/dot_general | solution.py:28
  360.7 5.1 %fusion.52 = f32[16,64,2,3,128]{4,0,3,2,1:T(8,128)S(1)} fusion(f32[16,64,2,3,128]{4,0,3,2,1:T(8,128)S(1)} %copy-done, f32[16,64,2,3,128]{4,1,0,3,2:T(8,128)S(1)} %bitcast.154), kind=kOutput, calls=%fused_computation.53 | convolution fusion | flops 151784960 | bytes 9437184 | tf_op jit(solution)/shard_map/dot_general | solution.py:28
  370.5 31.4 %all_to_all.30 = f32[1024,3,128]{2,1,0:T(4,128)S(1)} all-to-all(f32[1024,3,128]{2,1,0:T(4,128)S(1)} %copy.155), channel_id=1, replica_groups=mesh['ctx'=16,'ch'=8] {'ctx'}, dimensions={0} | all-to-all | bytes 3145728 | tf_op jit(solution)/shard_map/all_to_all | solution.py:165
  (80 shorter events, 72.8 us)
Async XLA Ops:
  1.3 4.8 %collective-permute-start = (bf16[3,2,128]{2,1,0:T(2,128)(2,1)S(1)}, bf16[3,2,128]{2,1,0:T(2,128)(2,1)S(1)}, u32[]{:S(2)}, u32[]{:S(2)}) collective-permute-start(bf16[3,2,128]{2,1,0:T(2,128)(2,1)S(1)} %slice.67), channel_id=1, source_target_pairs={{0,8},{8,16},{16,24},{24,32},{32,40},{40,48},{48,56},{56,64},{64,7... | collective-permute-start | bytes 4616 | tf_op jit(solution)/shard_map/ppermute | solution.py:12
  7.4 1.0 copy-start.4
  7.4 1.1 copy-start.5
  11.2 37.3 %all-to-all-start = ((f32[1024,3,128]{2,1,0:T(4,128)}), f32[1024,3,128]{2,1,0:T(4,128)}, u32[]{:S(2)}, u32[]{:S(2)}) async-start(f32[1024,3,128]{2,1,0:T(4,128)} %pad_maximum_fusion.2), calls=%async_computation | async-start | bytes 4194304 | tf_op jit(solution)/shard_map/all_to_all | solution.py:144
  73.0 48.0 %all-to-all-start.2 = ((f32[1024,2,3,128]{3,1,2,0:T(2,128)}), f32[1024,2,3,128]{3,1,2,0:T(2,128)}, u32[]{:S(2)}, u32[]{:S(2)}) async-start(f32[1024,2,3,128]{3,1,2,0:T(2,128)} %copy.121), calls=%async_computation.2 | async-start | bytes 6291456 | tf_op jit(solution)/shard_map/all_to_all | solution.py:152
  121.1 47.2 %all-to-all-start.1 = ((f32[1024,2,3,128]{3,1,2,0:T(2,128)}), f32[1024,2,3,128]{3,1,2,0:T(2,128)}, u32[]{:S(2)}, u32[]{:S(2)}) async-start(f32[1024,2,3,128]{3,1,2,0:T(2,128)} %copy.118), calls=%async_computation.1 | async-start | bytes 6291456 | tf_op jit(solution)/shard_map/all_to_all | solution.py:151
  168.3 2.8 copy-start.1
  171.1 5.8 %copy-start.2 = (f32[32,32,2,3,128]{4,0,3,2,1:T(8,128)S(1)}, f32[32,32,2,3,128]{4,0,3,2,1:T(8,128)}, u32[]{:S(2)}) copy-start(f32[32,32,2,3,128]{4,0,3,2,1:T(8,128)} %fusion.26) | copy-start | bytes 9437188
  258.0 48.0 %all-to-all-start.4 = ((f32[1024,2,3,128]{3,1,2,0:T(2,128)}), f32[1024,2,3,128]{3,1,2,0:T(2,128)}, u32[]{:S(2)}, u32[]{:S(2)}) async-start(f32[1024,2,3,128]{3,1,2,0:T(2,128)} %copy.147), calls=%async_computation.4 | async-start | bytes 6291456 | tf_op jit(solution)/shard_map/all_to_all | solution.py:158
  306.0 47.3 %all-to-all-start.3 = ((f32[1024,2,3,128]{3,1,2,0:T(2,128)}), f32[1024,2,3,128]{3,1,2,0:T(2,128)}, u32[]{:S(2)}, u32[]{:S(2)}) async-start(f32[1024,2,3,128]{3,1,2,0:T(2,128)} %copy.144), calls=%async_computation.3 | async-start | bytes 6291456 | tf_op jit(solution)/shard_map/all_to_all | solution.py:157
  355.4 5.3 %copy-start = (f32[16,64,2,3,128]{4,0,3,2,1:T(8,128)S(1)}, f32[16,64,2,3,128]{4,0,3,2,1:T(8,128)}, u32[]{:S(2)}) copy-start(f32[16,64,2,3,128]{4,0,3,2,1:T(8,128)} %fusion.4) | copy-start | bytes 9437188
  366.1 1.9 copy-start.3
where the time goes:
time: 410 us; the launch traced here: 406 us
  waiting for transfers between devices  158 us (39%)
  matrix products  120 us (29%)
  local copies, waits for them, and re-layouts  50.5 us (12%)
  blocking collectives  31.4 us (8%)
  starting transfers between devices  30.2 us (7%)
  other arithmetic  15.4 us (4%)
    dot_general x26, matrix products, mixing(): jnp.tensordot(table_part, values_in, axes=((0,), (along_axis,)), precisio...  120 us
    all_to_all x2, waiting for transfers between devices, along_context(): lax.all_to_all(imag_part, 'ctx', split_axis=0, concat_axis=0, tiled=True)  75.1 us
    all_to_all x2, waiting for transfers between devices, along_context(): lax.all_to_all(real_part, 'ctx', split_axis=0, concat_axis=0, tiled=True)  53.7 us
    all_to_all x1, blocking collectives, along_context(): lax.all_to_all(merged, 'ctx', split_axis=0, concat_axis=0, tiled=True)  31.4 us
    all_to_all x1, waiting for transfers between devices, along_context(): lax.all_to_all(signals, 'ctx', split_axis=0, concat_axis=0, tiled=True)  28.4 us
    sub x2, local copies, waits for them, and re-layouts, rotate(): real_part * cosine - imag_part * sine_part  11.9 us
    all_to_all x2, starting transfers between devices, along_context(): lax.all_to_all(real_part, 'ctx', split_axis=0, concat_axis=0, tiled=True)  9.38 us
    all_to_all x2, starting transfers between devices, along_context(): lax.all_to_all(imag_part, 'ctx', split_axis=0, concat_axis=0, tiled=True)  8.97 us
  transfers between devices with their start and end apart: 6, of which 6 were waited for; matrix products, arithmetic and copies ran while one was open for 11% of the time, Pallas kernels for 0%

commit v1 on v0

v1 whole, which is shorter than its diff:
```python
import math

import jax
import jax.numpy as jnp
import ml_dtypes
import numpy as np
from jax import lax
from jax.experimental import pallas as pl
from jax.experimental.pallas import tpu as pltpu
from jax.sharding import PartitionSpec as P

MESH = pl.DeviceIdType.MESH
SIDE = 128
DEVICES = 16
SUB = 8
BLOCKS = 8
F32, BF16 = jnp.float32, jnp.bfloat16


def halves(table):
    high = table.astype(ml_dtypes.bfloat16)
    low = (table - high.astype(np.float64)).astype(ml_dtypes.bfloat16)
    return high, low


def tables():
    index = np.arange(SIDE)
    outer = 2.0 * math.pi * ((4 * index[:, None] + 1) * index[None, :] % (4 * SIDE)) / (4 * SIDE)
    inner = 2.0 * math.pi * (index[:, None] * index[None, :] % SIDE) / SIDE
    turn = 2.0 * math.pi * ((4 * index[:, None] + 1) * index[None, :]) / (4 * SIDE * SIDE)
    first = np.concatenate([np.cos(outer), -np.sin(outer)], axis=0)
    cos, sin = np.cos(inner), np.sin(inner)
    second = np.block([[cos, -sin], [sin, cos]])
    back = np.block([[cos, sin], [-sin, cos]])
    last = np.concatenate([np.cos(outer).T, -np.sin(outer).T], axis=1) / (SIDE * SIDE)
    twist = np.stack([np.cos(turn), np.sin(turn)]).astype(np.float32)
    return halves(first) + halves(second) + halves(back) + halves(last) + (twist,)


def split(value):
    high = value.astype(BF16)
    return high, (value - high.astype(F32)).astype(BF16)


def dot(left, right):
    return jnp.dot(left, right, preferred_element_type=F32)


def left_product(high_ref, low_ref, value):
    high, low = split(value)
    return dot(high_ref[...], high) + dot(high_ref[...], low) + dot(low_ref[...], high)


def right_product(value, high_ref, low_ref):
    high, low = split(value)
    return dot(high, high_ref[...]) + dot(low, high_ref[...]) + dot(high, low_ref[...])


def kernel(
    proj, taps, filt, grad, first_h, first_l, second_h, second_l, back_h, back_l, last_h, last_l, twist,
    mixed, grad_streams, grad_filter,
    sent, got, made, home, streams, halo, spectra, send_sem, recv_sem, halo_sem,
):
    me = lax.axis_index("ctx")
    row, column = me // 4, me % 4

    def peer_of(step):
        return (row + step // 4) % 4 * 4 + (column + step % 4) % 4

    def copy_to(message, source, target, peer):
        return pltpu.make_async_remote_copy(
            src_ref=source.at[peer], dst_ref=target.at[me],
            send_sem=send_sem.at[message, peer], recv_sem=recv_sem.at[message, me],
            device_id={"ctx": peer}, device_id_type=MESH,
        )

    def copy_from(message, source, target, peer):
        return pltpu.make_async_remote_copy(
            src_ref=source.at[peer], dst_ref=target.at[peer],
            send_sem=send_sem.at[message, peer], recv_sem=recv_sem.at[message, peer],
            device_id={"ctx": peer}, device_id_type=MESH,
        )

    def each_peer(action):
        def body(step, carry):
            action(peer_of(step))
            return carry
        lax.fori_loop(1, DEVICES, body, 0)

    pairs = [(sent.at[m], got.at[m]) for m in range(3)] + [(made.at[m], home.at[m]) for m in range(3)]

    def send(message):
        source, target = pairs[message]
        each_peer(lambda peer: copy_to(message, source, target, peer).start())
        target[me] = source[me]

    def receive(message):
        source, target = pairs[message]
        each_peer(lambda peer: copy_from(message, source, target, peer).wait_recv())

    def rows_of(block):
        return pl.ds(pl.multiple_of(block * SIDE, SIDE), SIDE)

    def turned_out(message, block, value):
        sent[message, :, pl.ds(pl.multiple_of(block * SUB, SUB), SUB), :] = value.T.reshape(DEVICES, SUB, SIDE)

    def turned_home(message, block):
        return home[message, :, pl.ds(pl.multiple_of(block * SUB, SUB), SUB), :].reshape(SIDE, SIDE).T

    barrier = pltpu.get_barrier_semaphore()
    each_peer(lambda peer: pl.semaphore_signal(barrier, inc=1, device_id={"ctx": peer}, device_id_type=MESH))

    def filter_block(block, carry):
        turned_out(0, block, filt[rows_of(block), :])
        return carry
    lax.fori_loop(0, BLOCKS, filter_block, 0)

    pl.semaphore_wait(barrier, DEVICES - 1)
    after, before = (me + 1) % DEVICES, (me + DEVICES - 1) % DEVICES
    tail = pl.ds(BLOCKS * SIDE - 16, 16)

    def halo_copy(peer):
        return pltpu.make_async_remote_copy(
            src_ref=proj.at[:, tail, :], dst_ref=halo, send_sem=halo_sem.at[0], recv_sem=halo_sem.at[1],
            device_id={"ctx": peer}, device_id_type=MESH,
        )

    halo_copy(after).start()
    send(0)

    def short(stream, block, previous):
        now = proj[stream, rows_of(block), :].astype(F32)
        window = jnp.concatenate([previous[8:], now], axis=0)
        value = (
            taps[stream, 0:1, :] * now
            + taps[stream, 1:2, :] * window[7 : 7 + SIDE]
            + taps[stream, 2:3, :] * window[6 : 6 + SIDE]
        )
        streams[stream, rows_of(block), :] = value
        return value

    def inside(stream, block):
        return proj[stream, pl.ds(pl.multiple_of(block * SIDE - 16, 16), 16), :].astype(F32)

    def edge(stream):
        return jnp.where(me > 0, halo[stream].astype(F32), 0.0)

    def key_value(block, previous):
        turned_out(1, block, short(1, block, previous(1)) * short(2, block, previous(2)))

    def back_gated(block, previous):
        turned_out(2, block, short(0, block, previous(0)) * grad[rows_of(block), :].astype(F32))

    def later_blocks(make):
        def body(block, carry):
            make(block, lambda stream: inside(stream, block))
            return carry
        lax.fori_loop(1, BLOCKS, body, 0)

    later_blocks(key_value)
    halo_copy(before).wait_recv()
    key_value(0, edge)
    send(1)
    later_blocks(back_gated)
    back_gated(0, edge)
    send(2)

    def forward(message, pair):
        parts = [
            got[message, :, pl.ds(2 * pair + i, SUB, stride=SUB), :].reshape(SIDE, SIDE) for i in range(2)
        ]
        mixed_rows = left_product(first_h, first_l, jnp.concatenate(parts, axis=1))
        cos, sin = twist[0], twist[1]
        rows = []
        for i in range(2):
            real = mixed_rows[:SIDE, i * SIDE : (i + 1) * SIDE]
            imag = mixed_rows[SIDE:, i * SIDE : (i + 1) * SIDE]
            rows.append(jnp.concatenate([real * cos + imag * sin, imag * cos - real * sin], axis=1))
        return right_product(jnp.concatenate(rows, axis=0), second_h, second_l)

    def inverse(message, pair, real, imag):
        value = right_product(jnp.concatenate([real, imag], axis=1), back_h, back_l)
        cos, sin = twist[0], twist[1]
        columns = []
        for i in range(2):
            real = value[i * SIDE : (i + 1) * SIDE, :SIDE]
            imag = value[i * SIDE : (i + 1) * SIDE, SIDE:]
            columns.append(jnp.concatenate([real * cos - imag * sin, real * sin + imag * cos], axis=0))
        result = left_product(last_h, last_l, jnp.concatenate(columns, axis=1))
        for i in range(2):
            made[message, :, pl.ds(2 * pair + i, SUB, stride=SUB), :] = result[:, i * SIDE : (i + 1) * SIDE].reshape(
                DEVICES, SUB, SIDE
            )

    def parts_of(value):
        return value[:, :SIDE], value[:, SIDE:]

    def each_pair(action):
        def body(pair, carry):
            action(pair)
            return carry
        lax.fori_loop(0, SUB // 2, body, 0)

    def filter_pair(pair):
        spectra[0, pair] = forward(0, pair)

    def conv_pair(pair):
        value = forward(1, pair)
        spectra[1, pair] = value
        (fr, fi), (vr, vi) = parts_of(spectra[0, pair]), parts_of(value)
        inverse(0, pair, fr * vr - fi * vi, fr * vi + fi * vr)

    def stream_pair(pair):
        value = forward(2, pair)
        spectra[2, pair] = value
        (fr, fi), (br, bi) = parts_of(spectra[0, pair]), parts_of(value)
        inverse(1, pair, fr * br + fi * bi, fr * bi - fi * br)

    def filt_pair(pair):
        (vr, vi), (br, bi) = parts_of(spectra[1, pair]), parts_of(spectra[2, pair])
        inverse(2, pair, vr * br + vi * bi, vr * bi - vi * br)

    receive(0)
    each_pair(filter_pair)
    receive(1)
    each_pair(conv_pair)
    send(3)
    receive(2)
    each_pair(stream_pair)
    send(4)
    each_pair(filt_pair)
    send(5)

    def each_block(action):
        def body(block, carry):
            action(block)
            return carry
        lax.fori_loop(0, BLOCKS, body, 0)

    def conv_home(block):
        value, rows = turned_home(0, block), rows_of(block)
        mixed[rows, :] = (streams[0, rows, :] * value).astype(BF16)
        grad_streams[0, rows, :] = (grad[rows, :].astype(F32) * value).astype(BF16)

    def stream_home(block):
        value, rows = turned_home(1, block), rows_of(block)
        grad_streams[1, rows, :] = (value * streams[2, rows, :]).astype(BF16)
        grad_streams[2, rows, :] = (value * streams[1, rows, :]).astype(BF16)

    def filt_home(block):
        grad_filter[rows_of(block), :] = turned_home(2, block) * (1.0 / SIDE)

    for message, action in ((3, conv_home), (4, stream_home), (5, filt_home)):
        receive(message)
        each_block(action)
    for message in range(6):
        source, target = pairs[message]
        each_peer(lambda peer: copy_to(message, source, target, peer).wait_send())
    halo_copy(after).wait_send()


def local(projected, short_taps, long_filter, grad_mixed):
    constants = tables()
    tokens, channels = grad_mixed.shape
    in_vmem = pl.BlockSpec(memory_space=pltpu.VMEM)
    buffer = pltpu.VMEM((3, DEVICES, SUB * BLOCKS, SIDE), F32)
    return pl.pallas_call(
        kernel,
        out_shape=(
            jax.ShapeDtypeStruct((tokens, channels), BF16),
            jax.ShapeDtypeStruct((3, tokens, channels), BF16),
            jax.ShapeDtypeStruct((tokens, channels), F32),
        ),
        in_specs=[in_vmem] * (4 + len(constants)),
        out_specs=(in_vmem,) * 3,
        scratch_shapes=[
            buffer, buffer, buffer, buffer,
            pltpu.VMEM((3, tokens, channels), F32),
            pltpu.VMEM((3, 16, channels), BF16),
            pltpu.VMEM((3, SUB // 2, 2 * SIDE, 2 * SIDE), F32),
            pltpu.SemaphoreType.DMA((6, DEVICES)),
            pltpu.SemaphoreType.DMA((6, DEVICES)),
            pltpu.SemaphoreType.DMA((2,)),
        ],
        compiler_params=pltpu.CompilerParams(
            collective_id=0, has_side_effects=True, vmem_limit_bytes=48 * 1024 * 1024
        ),
    )(projected, short_taps, long_filter, grad_mixed, *[jnp.asarray(table) for table in constants])


def solution(mesh):
    in_specs = (P(None, "ctx", "ch"), P(None, None, "ch"), P("ctx", "ch"), P("ctx", "ch"))
    out_specs = (P("ctx", "ch"), P(None, "ctx", "ch"), P("ctx", "ch"))
    return jax.shard_map(local, mesh=mesh, in_specs=in_specs, out_specs=out_specs, check_vma=False)
```

time: 410 us -> 63.6 us (0.16)
  waiting for transfers between devices: 158 us -> 0 us
  matrix products: 120 us -> 0 us
  Pallas kernels: 0 us -> 48.3 us
  local copies, waits for them, and re-layouts: 50.5 us -> 14.1 us
  blocking collectives: 31.4 us -> 0 us
  starting transfers between devices: 30.2 us -> 0 us
  other arithmetic: 15.4 us -> 0 us
    all_to_all x5 -> x0, waiting for transfers between devices: 157 us -> none  [the longest x2 75.1 us: along_context(): lax.all_to_all(imag_part, 'ctx', split_axis=0, concat_axis=0, tiled=True)]
    dot_general x26 -> x0, matrix products: 120 us -> none  [mixing(): jnp.tensordot(table_part, values_in, axes=((0,), (along_axis,)), precisio...]
    pallas_call x0 -> x1, Pallas kernels: none -> 48.3 us  [local(): pl.pallas_call(kernel, out_shape=(jax.ShapeDtypeStruct((tokens, channels)...]
    all_to_all x1 -> x0, blocking collectives: 31.4 us -> none  [along_context(): lax.all_to_all(merged, 'ctx', split_axis=0, concat_axis=0, tiled=True)]
    all_to_all x5 -> x0, starting transfers between devices: 26.7 us -> none  [the longest x2 9.38 us: along_context(): lax.all_to_all(real_part, 'ctx', split_axis=0, concat_axis=0, tiled=True)]
    sub x5 -> x0, local copies, waits for them, and re-layouts: 16 us -> none  [the longest x2 11.9 us: rotate(): real_part * cosine - imag_part * sine_part]
    add x9 -> x0, local copies, waits for them, and re-layouts: 12.5 us -> none  [the longest x2 8.2 us: rotate(): real_part * sine_part + imag_part * cosine]
    all_to_all x5 -> x0, local copies, waits for them, and re-layouts: 10.2 us -> none  [the longest x2 4.33 us: along_context(): lax.all_to_all(real_part, 'ctx', split_axis=0, concat_axis=0, tiled=True)]
  transfers between devices with their start and end apart: 6 -> 0, of which waited for: 6 -> 0; matrix products, arithmetic and copies ran while one was open for 11% -> 0% of each run, Pallas kernels for 0% -> 0%
where the time goes in v1:
time: 63.6 us; the launch traced here: 63 us
  Pallas kernels  48.3 us (76%)
  local copies, waits for them, and re-layouts  14.1 us (22%)
  between operations  0.66 us (1%)
    pallas_call x1, Pallas kernels, local(): pl.pallas_call(kernel, out_shape=(jax.ShapeDtypeStruct((tokens, channels)...  48.3 us
    unnamed x29, local copies, waits for them, and re-layouts  14.1 us

profile of v1, /device:TPU:0, one launch (start us, length us, event | category | flops | bytes accessed | tf_op | source)
XLA Modules:
  0.0 63.0 jit_solution(6932502058610999532)
XLA Ops:
  0.6 0.0 copy-start
  0.6 1.1 %copy-done = bf16[3,1024,128]{2,1,0:T(8,128)(2,1)S(1)} copy-done((bf16[3,1024,128]{2,1,0:T(8,128)(2,1)S(1)}, bf16[3,1024,128]{2,1,0:T(8,128)(2,1)}, u32[]{:S(2)}) %copy-start) | copy-done | bytes 786456
  1.8 0.0 copy-start.1
  1.8 1.0 %copy-done.1 = f32[1024,128]{1,0:T(8,128)S(1)} copy-done((f32[1024,128]{1,0:T(8,128)S(1)}, f32[1024,128]{1,0:T(8,128)}, u32[]{:S(2)}) %copy-start.1) | copy-done | bytes 524312
  2.8 0.0 copy-start.2
  2.8 0.9 %copy-done.2 = bf16[1024,128]{1,0:T(8,128)(2,1)S(1)} copy-done((bf16[1024,128]{1,0:T(8,128)(2,1)S(1)}, bf16[1024,128]{1,0:T(8,128)(2,1)}, u32[]{:S(2)}) %copy-start.2) | copy-done | bytes 262168
  3.8 0.0 copy-start.3
  3.8 0.9 %copy-done.3 = f32[2,128,128]{2,1,0:T(8,128)S(1)} copy-done((f32[2,128,128]{2,1,0:T(8,128)S(1)}, f32[2,128,128]{2,1,0:T(8,128)}, u32[]{:S(2)}) %copy-start.3) | copy-done | bytes 131096
  4.7 0.0 copy-start.4
  4.7 0.9 %copy-done.4 = bf16[256,256]{1,0:T(8,128)(2,1)S(1)} copy-done((bf16[256,256]{1,0:T(8,128)(2,1)S(1)}, bf16[256,256]{1,0:T(8,128)(2,1)}, u32[]{:S(2)}) %copy-start.4) | copy-done | bytes 131096
  5.6 0.0 copy-start.5
  5.6 0.9 %copy-done.5 = bf16[256,256]{1,0:T(8,128)(2,1)S(1)} copy-done((bf16[256,256]{1,0:T(8,128)(2,1)S(1)}, bf16[256,256]{1,0:T(8,128)(2,1)}, u32[]{:S(2)}) %copy-start.5) | copy-done | bytes 131096
  6.5 0.0 copy-start.6
  6.5 0.9 %copy-done.6 = bf16[256,256]{1,0:T(8,128)(2,1)S(1)} copy-done((bf16[256,256]{1,0:T(8,128)(2,1)S(1)}, bf16[256,256]{1,0:T(8,128)(2,1)}, u32[]{:S(2)}) %copy-start.6) | copy-done | bytes 131096
  7.4 0.0 copy-start.7
  7.4 0.9 %copy-done.7 = bf16[256,256]{1,0:T(8,128)(2,1)S(1)} copy-done((bf16[256,256]{1,0:T(8,128)(2,1)S(1)}, bf16[256,256]{1,0:T(8,128)(2,1)}, u32[]{:S(2)}) %copy-start.7) | copy-done | bytes 131096
  8.3 0.0 copy-start.8
  8.3 0.8 %copy-done.8 = bf16[128,256]{1,0:T(8,128)(2,1)S(1)} copy-done((bf16[128,256]{1,0:T(8,128)(2,1)S(1)}, bf16[128,256]{1,0:T(8,128)(2,1)}, u32[]{:S(2)}) %copy-start.8) | copy-done | bytes 65560
  9.1 0.0 copy-start.9
  9.1 0.8 %copy-done.9 = bf16[128,256]{1,0:T(8,128)(2,1)S(1)} copy-done((bf16[128,256]{1,0:T(8,128)(2,1)S(1)}, bf16[128,256]{1,0:T(8,128)(2,1)}, u32[]{:S(2)}) %copy-start.9) | copy-done | bytes 65560
  10.0 0.0 copy-start.10
  10.0 0.8 %copy-done.10 = bf16[256,128]{1,0:T(8,128)(2,1)S(1)} copy-done((bf16[256,128]{1,0:T(8,128)(2,1)S(1)}, bf16[256,128]{1,0:T(8,128)(2,1)}, u32[]{:S(2)}) %copy-start.10) | copy-done | bytes 65560
  10.8 0.0 copy-start.11
  10.8 0.8 %copy-done.11 = bf16[256,128]{1,0:T(8,128)(2,1)S(1)} copy-done((bf16[256,128]{1,0:T(8,128)(2,1)S(1)}, bf16[256,128]{1,0:T(8,128)(2,1)}, u32[]{:S(2)}) %copy-start.11) | copy-done | bytes 65560
  11.6 0.0 copy-start.12
  11.6 0.7 %copy-done.12 = f32[3,3,128]{2,1,0:T(4,128)S(1)} copy-done((f32[3,3,128]{2,1,0:T(4,128)S(1)}, f32[3,3,128]{2,1,0:T(4,128)}, u32[]{:S(2)}) %copy-start.12) | copy-done | bytes 4632
  12.3 48.3 %shard_map.148 = (bf16[1024,128]{1,0:T(8,128)(2,1)S(1)}, bf16[3,1024,128]{2,1,0:T(8,128)(2,1)S(1)}, f32[1024,128]{1,0:T(8,128)S(1)}) custom-call(bf16[3,1024,128]{2,1,0:T(8,128)(2,1)S(1)} %copy-done, f32[3,3,128]{2,1,0:T(4,128)S(1)} %copy-done.12, f32[1024,128]{1,0:T(8,128)S(1)} %copy-done.1, bf16[1024,128]{1,0:T(8,128)(2,1)S(1)} %copy-done.2, ...), custom_call_target="tpu_custom_call" | custom-call | tf_op jit(solution)/shard_map/pallas_call | solution.py:267
  60.7 0.7 %copy.19 = bf16[1024,128]{1,0:T(8,128)(2,1)} copy(bf16[1024,128]{1,0:T(8,128)(2,1)S(1)} %get-tuple-element.6) | data formatting | bytes 524288
  61.4 0.9 %copy.20 = bf16[3,1024,128]{2,1,0:T(8,128)(2,1)} copy(bf16[3,1024,128]{2,1,0:T(8,128)(2,1)S(1)} %get-tuple-element.7) | data formatting | bytes 1572864
  62.2 0.8 %copy.21 = f32[1024,128]{1,0:T(8,128)} copy(f32[1024,128]{1,0:T(8,128)S(1)} %get-tuple-element.8) | data formatting | bytes 1048576
Async XLA Ops:
  0.6 1.1 %copy-start = (bf16[3,1024,128]{2,1,0:T(8,128)(2,1)S(1)}, bf16[3,1024,128]{2,1,0:T(8,128)(2,1)}, u32[]{:S(2)}) copy-start(bf16[3,1024,128]{2,1,0:T(8,128)(2,1)} %proj.1) | copy-start | bytes 2359300
  1.8 1.0 %copy-start.1 = (f32[1024,128]{1,0:T(8,128)S(1)}, f32[1024,128]{1,0:T(8,128)}, u32[]{:S(2)}) copy-start(f32[1024,128]{1,0:T(8,128)} %filt.1) | copy-start | bytes 1572868
  2.8 0.9 %copy-start.2 = (bf16[1024,128]{1,0:T(8,128)(2,1)S(1)}, bf16[1024,128]{1,0:T(8,128)(2,1)}, u32[]{:S(2)}) copy-start(bf16[1024,128]{1,0:T(8,128)(2,1)} %grad.1) | copy-start | bytes 786436
  3.8 0.9 %copy-start.3 = (f32[2,128,128]{2,1,0:T(8,128)S(1)}, f32[2,128,128]{2,1,0:T(8,128)}, u32[]{:S(2)}) copy-start(f32[2,128,128]{2,1,0:T(8,128)} %constant.26.clone.twist) | copy-start | bytes 393220
  4.7 0.9 %copy-start.4 = (bf16[256,256]{1,0:T(8,128)(2,1)S(1)}, bf16[256,256]{1,0:T(8,128)(2,1)}, u32[]{:S(2)}) copy-start(bf16[256,256]{1,0:T(8,128)(2,1)} %constant.23.clone.back_l) | copy-start | bytes 393220
  5.6 0.9 %copy-start.5 = (bf16[256,256]{1,0:T(8,128)(2,1)S(1)}, bf16[256,256]{1,0:T(8,128)(2,1)}, u32[]{:S(2)}) copy-start(bf16[256,256]{1,0:T(8,128)(2,1)} %constant.22.clone.back_h) | copy-start | bytes 393220
  6.5 0.9 %copy-start.6 = (bf16[256,256]{1,0:T(8,128)(2,1)S(1)}, bf16[256,256]{1,0:T(8,128)(2,1)}, u32[]{:S(2)}) copy-start(bf16[256,256]{1,0:T(8,128)(2,1)} %constant.21.clone.second_l) | copy-start | bytes 393220
  7.4 0.9 %copy-start.7 = (bf16[256,256]{1,0:T(8,128)(2,1)S(1)}, bf16[256,256]{1,0:T(8,128)(2,1)}, u32[]{:S(2)}) copy-start(bf16[256,256]{1,0:T(8,128)(2,1)} %constant.20.clone.second_h) | copy-start | bytes 393220
  8.3 0.8 %copy-start.8 = (bf16[128,256]{1,0:T(8,128)(2,1)S(1)}, bf16[128,256]{1,0:T(8,128)(2,1)}, u32[]{:S(2)}) copy-start(bf16[128,256]{1,0:T(8,128)(2,1)} %constant.25.clone.last_l) | copy-start | bytes 196612
  9.1 0.8 %copy-start.9 = (bf16[128,256]{1,0:T(8,128)(2,1)S(1)}, bf16[128,256]{1,0:T(8,128)(2,1)}, u32[]{:S(2)}) copy-start(bf16[128,256]{1,0:T(8,128)(2,1)} %constant.24.clone.last_h) | copy-start | bytes 196612
  10.0 0.8 %copy-start.10 = (bf16[256,128]{1,0:T(8,128)(2,1)S(1)}, bf16[256,128]{1,0:T(8,128)(2,1)}, u32[]{:S(2)}) copy-start(bf16[256,128]{1,0:T(8,128)(2,1)} %constant.19.clone.first_l) | copy-start | bytes 196612
  10.8 0.8 %copy-start.11 = (bf16[256,128]{1,0:T(8,128)(2,1)S(1)}, bf16[256,128]{1,0:T(8,128)(2,1)}, u32[]{:S(2)}) copy-start(bf16[256,128]{1,0:T(8,128)(2,1)} %constant.18.clone.first_h) | copy-start | bytes 196612
  11.6 0.7 %copy-start.12 = (f32[3,3,128]{2,1,0:T(4,128)S(1)}, f32[3,3,128]{2,1,0:T(4,128)}, u32[]{:S(2)}) copy-start(f32[3,3,128]{2,1,0:T(4,128)} %taps.1) | copy-start | bytes 13828

commit v2 on v1

--- a/solution.py
+++ b/solution.py
@@ -34,7 +34,7 @@
     back = np.block([[cos, sin], [-sin, cos]])
     last = np.concatenate([np.cos(outer).T, -np.sin(outer).T], axis=1) / (SIDE * SIDE)
     twist = np.stack([np.cos(turn), np.sin(turn)]).astype(np.float32)
-    return halves(first) + halves(second) + halves(back) + halves(last) + (twist,)
+    return np.stack(halves(first)), np.stack(halves(second)), np.stack(halves(back)), np.stack(halves(last)), twist
 
 
 def split(value):
@@ -46,21 +46,31 @@
     return jnp.dot(left, right, preferred_element_type=F32)
 
 
-def left_product(high_ref, low_ref, value):
+def left_product(table, value):
     high, low = split(value)
-    return dot(high_ref[...], high) + dot(high_ref[...], low) + dot(low_ref[...], high)
-
-
-def right_product(value, high_ref, low_ref):
+    return dot(table[0], high) + dot(table[0], low) + dot(table[1], high)
+
+
+def right_product(value, table):
     high, low = split(value)
-    return dot(high, high_ref[...]) + dot(low, high_ref[...]) + dot(high, low_ref[...])
+    return dot(high, table[0]) + dot(low, table[0]) + dot(high, table[1])
 
 
 def kernel(
-    proj, taps, filt, grad, first_h, first_l, second_h, second_l, back_h, back_l, last_h, last_l, twist,
+    filt_hbm, proj_hbm, taps_hbm, grad_hbm, first_hbm, second_hbm, twist_hbm, back_hbm, last_hbm,
     mixed, grad_streams, grad_filter,
-    sent, got, made, home, streams, halo, spectra, send_sem, recv_sem, halo_sem,
+    filt, proj, taps, grad, first, second, twist, back, last,
+    sent, got, made, home, streams, halo, spectra, load_sem, send_sem, recv_sem, halo_sem,
 ):
+    loads = [
+        pltpu.make_async_copy(source, target, load_sem.at[i])
+        for i, (source, target) in enumerate((
+            (filt_hbm, filt), (proj_hbm, proj), (taps_hbm, taps), (grad_hbm, grad), (first_hbm, first),
+            (second_hbm, second), (twist_hbm, twist), (back_hbm, back), (last_hbm, last),
+        ))
+    ]
+    for load in loads:
+        load.start()
     me = lax.axis_index("ctx")
     row, column = me // 4, me % 4
 
@@ -110,12 +120,15 @@
     barrier = pltpu.get_barrier_semaphore()
     each_peer(lambda peer: pl.semaphore_signal(barrier, inc=1, device_id={"ctx": peer}, device_id_type=MESH))
 
+    loads[0].wait()
+
     def filter_block(block, carry):
         turned_out(0, block, filt[rows_of(block), :])
         return carry
     lax.fori_loop(0, BLOCKS, filter_block, 0)
 
     pl.semaphore_wait(barrier, DEVICES - 1)
+    loads[1].wait()
     after, before = (me + 1) % DEVICES, (me + DEVICES - 1) % DEVICES
     tail = pl.ds(BLOCKS * SIDE - 16, 16)
 
@@ -157,10 +170,12 @@
             return carry
         lax.fori_loop(1, BLOCKS, body, 0)
 
+    loads[2].wait()
     later_blocks(key_value)
     halo_copy(before).wait_recv()
     key_value(0, edge)
     send(1)
+    loads[3].wait()
     later_blocks(back_gated)
     back_gated(0, edge)
     send(2)
@@ -169,24 +184,24 @@
         parts = [
             got[message, :, pl.ds(2 * pair + i, SUB, stride=SUB), :].reshape(SIDE, SIDE) for i in range(2)
         ]
-        mixed_rows = left_product(first_h, first_l, jnp.concatenate(parts, axis=1))
+        mixed_rows = left_product(first, jnp.concatenate(parts, axis=1))
         cos, sin = twist[0], twist[1]
         rows = []
         for i in range(2):
             real = mixed_rows[:SIDE, i * SIDE : (i + 1) * SIDE]
             imag = mixed_rows[SIDE:, i * SIDE : (i + 1) * SIDE]
             rows.append(jnp.concatenate([real * cos + imag * sin, imag * cos - real * sin], axis=1))
-        return right_product(jnp.concatenate(rows, axis=0), second_h, second_l)
+        return right_product(jnp.concatenate(rows, axis=0), second)
 
     def inverse(message, pair, real, imag):
-        value = right_product(jnp.concatenate([real, imag], axis=1), back_h, back_l)
+        value = right_product(jnp.concatenate([real, imag], axis=1), back)
         cos, sin = twist[0], twist[1]
         columns = []
         for i in range(2):
             real = value[i * SIDE : (i + 1) * SIDE, :SIDE]
             imag = value[i * SIDE : (i + 1) * SIDE, SIDE:]
             columns.append(jnp.concatenate([real * cos - imag * sin, real * sin + imag * cos], axis=0))
-        result = left_product(last_h, last_l, jnp.concatenate(columns, axis=1))
+        result = left_product(last, jnp.concatenate(columns, axis=1))
         for i in range(2):
             made[message, :, pl.ds(2 * pair + i, SUB, stride=SUB), :] = result[:, i * SIDE : (i + 1) * SIDE].reshape(
                 DEVICES, SUB, SIDE
@@ -220,6 +235,8 @@
         (vr, vi), (br, bi) = parts_of(spectra[1, pair]), parts_of(spectra[2, pair])
         inverse(2, pair, vr * br + vi * bi, vr * bi - vi * br)
 
+    for load in loads[4:]:
+        load.wait()
     receive(0)
     each_pair(filter_pair)
     receive(1)
@@ -259,33 +276,58 @@
     halo_copy(after).wait_send()
 
 
+def write_out(mixed, grad_streams, grad_filter, mixed_hbm, grad_streams_hbm, grad_filter_hbm, sems):
+    copies = [
+        pltpu.make_async_copy(source, target, sems.at[i])
+        for i, (source, target) in enumerate((
+            (grad_streams, grad_streams_hbm), (grad_filter, grad_filter_hbm), (mixed, mixed_hbm),
+        ))
+    ]
+    for copy in copies:
+        copy.start()
+    for copy in copies:
+        copy.wait()
+
+
 def local(projected, short_taps, long_filter, grad_mixed):
-    constants = tables()
+    first, second, back, last, twist = (jnp.asarray(table) for table in tables())
+    operands = (long_filter, projected, short_taps, grad_mixed, first, second, twist, back, last)
     tokens, channels = grad_mixed.shape
     in_vmem = pl.BlockSpec(memory_space=pltpu.VMEM)
+    in_hbm = pl.BlockSpec(memory_space=pltpu.MemorySpace.HBM)
     buffer = pltpu.VMEM((3, DEVICES, SUB * BLOCKS, SIDE), F32)
-    return pl.pallas_call(
+    out_shape = (
+        jax.ShapeDtypeStruct((tokens, channels), BF16),
+        jax.ShapeDtypeStruct((3, tokens, channels), BF16),
+        jax.ShapeDtypeStruct((tokens, channels), F32),
+    )
+    results = pl.pallas_call(
         kernel,
-        out_shape=(
-            jax.ShapeDtypeStruct((tokens, channels), BF16),
-            jax.ShapeDtypeStruct((3, tokens, channels), BF16),
-            jax.ShapeDtypeStruct((tokens, channels), F32),
-        ),
-        in_specs=[in_vmem] * (4 + len(constants)),
+        out_shape=out_shape,
+        in_specs=[in_hbm] * len(operands),
         out_specs=(in_vmem,) * 3,
-        scratch_shapes=[
+        scratch_shapes=[pltpu.VMEM(operand.shape, operand.dtype) for operand in operands]
+        + [
             buffer, buffer, buffer, buffer,
             pltpu.VMEM((3, tokens, channels), F32),
             pltpu.VMEM((3, 16, channels), BF16),
             pltpu.VMEM((3, SUB // 2, 2 * SIDE, 2 * SIDE), F32),
+            pltpu.SemaphoreType.DMA((len(operands),)),
             pltpu.SemaphoreType.DMA((6, DEVICES)),
             pltpu.SemaphoreType.DMA((6, DEVICES)),
             pltpu.SemaphoreType.DMA((2,)),
         ],
         compiler_params=pltpu.CompilerParams(
-            collective_id=0, has_side_effects=True, vmem_limit_bytes=48 * 1024 * 1024
+            collective_id=0, has_side_effects=True, vmem_limit_bytes=40 * 1024 * 1024
         ),
-    )(projected, short_taps, long_filter, grad_mixed, *[jnp.asarray(table) for table in constants])
+    )(*[pltpu.with_memory_space_constraint(operand, pltpu.MemorySpace.HBM) for operand in operands])
+    return pl.pallas_call(
+        write_out,
+        out_shape=out_shape,
+        in_specs=[in_vmem] * 3,
+        out_specs=(in_hbm,) * 3,
+        scratch_shapes=[pltpu.SemaphoreType.DMA((3,))],
+    )(*[pltpu.with_memory_space_constraint(result, pltpu.VMEM) for result in results])
 
 
 def solution(mesh):

time: 63.6 us -> 50.6 us (0.80)
  local copies, waits for them, and re-layouts: 14.1 us -> 0 us
  Pallas kernels: 48.3 us -> 49.9 us
    unnamed x29 -> x0, local copies, waits for them, and re-layouts: 14.1 us -> none
    pallas_call x1 -> x2, Pallas kernels: 48.3 us -> 49.9 us  [the longest x1 48.7 us: local(): pl.pallas_call(kernel, out_shape=out_shape, in_specs=[in_hbm] * len(opera...]
where the time goes in v2:
time: 50.6 us; the launch traced here: 50.5 us
  Pallas kernels  49.9 us (99%)
  between operations  0.64 us (1%)
    pallas_call x1, Pallas kernels, local(): pl.pallas_call(kernel, out_shape=out_shape, in_specs=[in_hbm] * len(opera...  48.7 us
    pallas_call x1, Pallas kernels, local(): pl.pallas_call(write_out, out_shape=out_shape, in_specs=[in_vmem] * 3, ou...  1.16 us

profile of v2, /device:TPU:0, one launch (start us, length us, event | category | flops | bytes accessed | tf_op | source)
XLA Modules:
  0.0 50.5 jit_solution(8662289905108872815)
XLA Ops:
  0.6 48.7 %shard_map.112 = (bf16[1024,128]{1,0:T(8,128)(2,1)S(1)}, bf16[3,1024,128]{2,1,0:T(8,128)(2,1)S(1)}, f32[1024,128]{1,0:T(8,128)S(1)}) custom-call(f32[1024,128]{1,0:T(8,128)} %filt_hbm.1, bf16[3,1024,128]{2,1,0:T(8,128)(2,1)} %proj_hbm.1, f32[3,3,128]{2,1,0:T(4,128)} %taps_hbm.1, bf16[1024,128]{1,0:T(8,128)(2,1)} %grad_hbm.1, ...), custom_call_target="tpu_custom_call" | custom-call | tf_op jit(solution)/shard_map/pallas_call | solution.py:304
  49.4 1.2 %shard_map.113 = (bf16[1024,128]{1,0:T(8,128)(2,1)}, bf16[3,1024,128]{2,1,0:T(8,128)(2,1)}, f32[1024,128]{1,0:T(8,128)}) custom-call(bf16[1024,128]{1,0:T(8,128)(2,1)S(1)} %get-tuple-element.6.mixed, bf16[3,1024,128]{2,1,0:T(8,128)(2,1)S(1)} %get-tuple-element.7.grad_streams, f32[1024,128]{1,0:T(8,128)S(1)} %get-tuple-element.8.grad_filter), custom_call_target="tpu_custom_call" | custom-call | tf_op jit(solution)/shard_map/pallas_call | solution.py:324

commit v3 on v2

--- a/solution.py
+++ b/solution.py
@@ -14,6 +14,7 @@
 DEVICES = 16
 SUB = 8
 BLOCKS = 8
+OFFSET = 1.0 / 64.0
 F32, BF16 = jnp.float32, jnp.bfloat16
 
 
@@ -56,11 +57,32 @@
     return dot(high, table[0]) + dot(low, table[0]) + dot(high, table[1])
 
 
+def scale_of(largest):
+    return 8.0 / jnp.maximum(largest, 1e-30)
+
+
+def coded(value, scale):
+    base = jnp.abs(value) * scale + 8.0 * OFFSET
+    two = base * base
+    four = two * two
+    eight = four * four
+    sixteen = eight * eight
+    power = sixteen * sixteen * eight
+    return jnp.where(value < 0.0, -power, power)
+
+
+def decoded(code, largest):
+    root = jnp.exp2(jnp.log2(jnp.abs(code)) * (1.0 / 40.0))
+    size = root * (largest * 0.125) - largest * OFFSET
+    return jnp.where(code < 0.0, -size, size)
+
+
 def kernel(
     filt_hbm, proj_hbm, taps_hbm, grad_hbm, first_hbm, second_hbm, twist_hbm, back_hbm, last_hbm,
     mixed, grad_streams, grad_filter,
     filt, proj, taps, grad, first, second, twist, back, last,
-    sent, got, made, home, streams, halo, spectra, load_sem, send_sem, recv_sem, halo_sem,
+    sent, got, made, home, scales_out, scales_in, plain, gathered, results, streams, halo, spectra,
+    load_sem, send_sem, recv_sem, halo_sem,
 ):
     loads = [
         pltpu.make_async_copy(source, target, load_sem.at[i])
@@ -77,56 +99,68 @@
     def peer_of(step):
         return (row + step // 4) % 4 * 4 + (column + step % 4) % 4
 
-    def copy_to(message, source, target, peer):
+    def each_peer(action):
+        def body(step, carry):
+            action(peer_of(step))
+            return carry
+        lax.fori_loop(1, DEVICES, body, 0)
+
+    pairs = [(sent.at[m], got.at[m]) for m in range(3)] + [(made.at[m], home.at[m]) for m in range(3)]
+    pairs += [(scales_out.at[m], scales_in.at[m]) for m in range(6)]
+
+    def copy_to(message, peer):
+        source, target = pairs[message]
         return pltpu.make_async_remote_copy(
             src_ref=source.at[peer], dst_ref=target.at[me],
             send_sem=send_sem.at[message, peer], recv_sem=recv_sem.at[message, me],
             device_id={"ctx": peer}, device_id_type=MESH,
         )
 
-    def copy_from(message, source, target, peer):
+    def copy_from(message, peer):
+        source, target = pairs[message]
         return pltpu.make_async_remote_copy(
             src_ref=source.at[peer], dst_ref=target.at[peer],
             send_sem=send_sem.at[message, peer], recv_sem=recv_sem.at[message, peer],
             device_id={"ctx": peer}, device_id_type=MESH,
         )
 
-    def each_peer(action):
-        def body(step, carry):
-            action(peer_of(step))
-            return carry
-        lax.fori_loop(1, DEVICES, body, 0)
-
-    pairs = [(sent.at[m], got.at[m]) for m in range(3)] + [(made.at[m], home.at[m]) for m in range(3)]
-
     def send(message):
-        source, target = pairs[message]
-        each_peer(lambda peer: copy_to(message, source, target, peer).start())
-        target[me] = source[me]
+        def start(peer):
+            copy_to(message + 6, peer).start()
+            copy_to(message, peer).start()
+        each_peer(start)
+        for source, target in (pairs[message], pairs[message + 6]):
+            target[me] = source[me]
 
     def receive(message):
-        source, target = pairs[message]
-        each_peer(lambda peer: copy_from(message, source, target, peer).wait_recv())
+        def wait(peer):
+            copy_from(message + 6, peer).wait_recv()
+            copy_from(message, peer).wait_recv()
+        each_peer(wait)
 
     def rows_of(block):
         return pl.ds(pl.multiple_of(block * SIDE, SIDE), SIDE)
 
-    def turned_out(message, block, value):
-        sent[message, :, pl.ds(pl.multiple_of(block * SUB, SUB), SUB), :] = value.T.reshape(DEVICES, SUB, SIDE)
-
-    def turned_home(message, block):
-        return home[message, :, pl.ds(pl.multiple_of(block * SUB, SUB), SUB), :].reshape(SIDE, SIDE).T
+    def code_rows(pair):
+        return pl.ds(pl.multiple_of(pair * 2 * SUB, 2 * SUB), 2 * SUB)
+
+    def turned_out(message, source):
+        largest = jnp.max(jnp.abs(source[...]), axis=0, keepdims=True)
+        scales_out[message] = jnp.broadcast_to(largest[None], (DEVICES, 1, SIDE))
+        scale = scale_of(largest)
+
+        def body(pair, carry):
+            turned = [
+                coded(source[rows_of(2 * pair + i), :], scale).T.reshape(DEVICES, SUB, SIDE) for i in range(2)
+            ]
+            sent[message, :, code_rows(pair), :] = jnp.concatenate(turned, axis=1).astype(BF16)
+            return carry
+        lax.fori_loop(0, BLOCKS // 2, body, 0)
 
     barrier = pltpu.get_barrier_semaphore()
     each_peer(lambda peer: pl.semaphore_signal(barrier, inc=1, device_id={"ctx": peer}, device_id_type=MESH))
-
     loads[0].wait()
-
-    def filter_block(block, carry):
-        turned_out(0, block, filt[rows_of(block), :])
-        return carry
-    lax.fori_loop(0, BLOCKS, filter_block, 0)
-
+    turned_out(0, filt)
     pl.semaphore_wait(barrier, DEVICES - 1)
     loads[1].wait()
     after, before = (me + 1) % DEVICES, (me + DEVICES - 1) % DEVICES
@@ -159,10 +193,10 @@
         return jnp.where(me > 0, halo[stream].astype(F32), 0.0)
 
     def key_value(block, previous):
-        turned_out(1, block, short(1, block, previous(1)) * short(2, block, previous(2)))
+        plain[rows_of(block), :] = short(1, block, previous(1)) * short(2, block, previous(2))
 
     def back_gated(block, previous):
-        turned_out(2, block, short(0, block, previous(0)) * grad[rows_of(block), :].astype(F32))
+        plain[rows_of(block), :] = short(0, block, previous(0)) * grad[rows_of(block), :].astype(F32)
 
     def later_blocks(make):
         def body(block, carry):
@@ -174,16 +208,38 @@
     later_blocks(key_value)
     halo_copy(before).wait_recv()
     key_value(0, edge)
+    turned_out(1, plain)
     send(1)
     loads[3].wait()
     later_blocks(back_gated)
     back_gated(0, edge)
+    turned_out(2, plain)
     send(2)
 
-    def forward(message, pair):
-        parts = [
-            got[message, :, pl.ds(2 * pair + i, SUB, stride=SUB), :].reshape(SIDE, SIDE) for i in range(2)
-        ]
+    def lane_is_own(shape, axis):
+        lane = lax.broadcasted_iota(jnp.int32, shape, len(shape) - 1)
+        return lane == SUB * me + lax.broadcasted_iota(jnp.int32, shape, axis)
+
+    def gather(message):
+        receive(message)
+        shape = (DEVICES, SUB, SIDE)
+        rows = jnp.broadcast_to(scales_in[message], shape)
+        largest = jnp.sum(jnp.where(lane_is_own(shape, 1), rows, 0.0), axis=2, keepdims=True)
+        for source in range(DEVICES):
+            code = got[message, source].astype(F32).reshape(BLOCKS, SUB, SIDE)
+            gathered[source] = decoded(code, largest[source : source + 1]).reshape(BLOCKS * SUB, SIDE)
+
+    def scatter(message):
+        for target in range(DEVICES):
+            value = results[target].reshape(BLOCKS, SUB, SIDE)
+            largest = jnp.max(jnp.max(jnp.abs(value), axis=0), axis=1, keepdims=True)
+            spread = jnp.where(lane_is_own((SUB, SIDE), 0), largest, 0.0)
+            scales_out[message, target] = jnp.sum(spread, axis=0, keepdims=True)
+            made[message - 3, target] = coded(value, scale_of(largest)[None]).reshape(BLOCKS * SUB, SIDE).astype(BF16)
+        send(message)
+
+    def forward(pair):
+        parts = [gathered[:, pl.ds(2 * pair + i, SUB, stride=SUB), :].reshape(SIDE, SIDE) for i in range(2)]
         mixed_rows = left_product(first, jnp.concatenate(parts, axis=1))
         cos, sin = twist[0], twist[1]
         rows = []
@@ -193,7 +249,7 @@
             rows.append(jnp.concatenate([real * cos + imag * sin, imag * cos - real * sin], axis=1))
         return right_product(jnp.concatenate(rows, axis=0), second)
 
-    def inverse(message, pair, real, imag):
+    def inverse(pair, real, imag):
         value = right_product(jnp.concatenate([real, imag], axis=1), back)
         cos, sin = twist[0], twist[1]
         columns = []
@@ -203,7 +259,7 @@
             columns.append(jnp.concatenate([real * cos - imag * sin, real * sin + imag * cos], axis=0))
         result = left_product(last, jnp.concatenate(columns, axis=1))
         for i in range(2):
-            made[message, :, pl.ds(2 * pair + i, SUB, stride=SUB), :] = result[:, i * SIDE : (i + 1) * SIDE].reshape(
+            results[:, pl.ds(2 * pair + i, SUB, stride=SUB), :] = result[:, i * SIDE : (i + 1) * SIDE].reshape(
                 DEVICES, SUB, SIDE
             )
 
@@ -211,68 +267,69 @@
         return value[:, :SIDE], value[:, SIDE:]
 
     def each_pair(action):
-        def body(pair, carry):
+        for pair in range(SUB // 2):
             action(pair)
-            return carry
-        lax.fori_loop(0, SUB // 2, body, 0)
 
     def filter_pair(pair):
-        spectra[0, pair] = forward(0, pair)
+        spectra[0, pair] = forward(pair)
 
     def conv_pair(pair):
-        value = forward(1, pair)
+        value = forward(pair)
         spectra[1, pair] = value
         (fr, fi), (vr, vi) = parts_of(spectra[0, pair]), parts_of(value)
-        inverse(0, pair, fr * vr - fi * vi, fr * vi + fi * vr)
+        inverse(pair, fr * vr - fi * vi, fr * vi + fi * vr)
 
     def stream_pair(pair):
-        value = forward(2, pair)
+        value = forward(pair)
         spectra[2, pair] = value
         (fr, fi), (br, bi) = parts_of(spectra[0, pair]), parts_of(value)
-        inverse(1, pair, fr * br + fi * bi, fr * bi - fi * br)
+        inverse(pair, fr * br + fi * bi, fr * bi - fi * br)
 
     def filt_pair(pair):
         (vr, vi), (br, bi) = parts_of(spectra[1, pair]), parts_of(spectra[2, pair])
-        inverse(2, pair, vr * br + vi * bi, vr * bi - vi * br)
+        inverse(pair, vr * br + vi * bi, vr * bi - vi * br)
 
     for load in loads[4:]:
         load.wait()
-    receive(0)
+    gather(0)
     each_pair(filter_pair)
-    receive(1)
+    gather(1)
     each_pair(conv_pair)
-    send(3)
-    receive(2)
+    scatter(3)
+    gather(2)
     each_pair(stream_pair)
-    send(4)
+    scatter(4)
     each_pair(filt_pair)
-    send(5)
-
-    def each_block(action):
-        def body(block, carry):
-            action(block)
+    scatter(5)
+
+    def turned_home(message, action):
+        receive(message)
+        largest = jnp.sum(scales_in[message], axis=0)
+
+        def body(pair, carry):
+            code = home[message - 3, :, code_rows(pair), :].astype(F32)
+            for i in range(2):
+                turned = code[:, i * SUB : (i + 1) * SUB, :].reshape(SIDE, SIDE).T
+                action(rows_of(2 * pair + i), decoded(turned, largest))
             return carry
-        lax.fori_loop(0, BLOCKS, body, 0)
-
-    def conv_home(block):
-        value, rows = turned_home(0, block), rows_of(block)
+        lax.fori_loop(0, BLOCKS // 2, body, 0)
+
+    def conv_home(rows, value):
         mixed[rows, :] = (streams[0, rows, :] * value).astype(BF16)
         grad_streams[0, rows, :] = (grad[rows, :].astype(F32) * value).astype(BF16)
 
-    def stream_home(block):
-        value, rows = turned_home(1, block), rows_of(block)
+    def stream_home(rows, value):
         grad_streams[1, rows, :] = (value * streams[2, rows, :]).astype(BF16)
         grad_streams[2, rows, :] = (value * streams[1, rows, :]).astype(BF16)
 
-    def filt_home(block):
-        grad_filter[rows_of(block), :] = turned_home(2, block) * (1.0 / SIDE)
-
-    for message, action in ((3, conv_home), (4, stream_home), (5, filt_home)):
-        receive(message)
-        each_block(action)
-    for message in range(6):
-        source, target = pairs[message]
-        each_peer(lambda peer: copy_to(message, source, target, peer).wait_send())
+    def filt_home(rows, value):
+        grad_filter[rows, :] = value * (1.0 / SIDE)
+
+    turned_home(3, conv_home)
+    turned_home(4, stream_home)
+    turned_home(5, filt_home)
+    for message in range(12):
+        each_peer(lambda peer: copy_to(message, peer).wait_send())
     halo_copy(after).wait_send()
 
 
@@ -295,7 +352,9 @@
     tokens, channels = grad_mixed.shape
     in_vmem = pl.BlockSpec(memory_space=pltpu.VMEM)
     in_hbm = pl.BlockSpec(memory_space=pltpu.MemorySpace.HBM)
-    buffer = pltpu.VMEM((3, DEVICES, SUB * BLOCKS, SIDE), F32)
+    buffer = pltpu.VMEM((3, DEVICES, SUB * BLOCKS, SIDE), BF16)
+    scales = pltpu.VMEM((6, DEVICES, 1, SIDE), F32)
+    whole = pltpu.VMEM((DEVICES, SUB * BLOCKS, SIDE), F32)
     out_shape = (
         jax.ShapeDtypeStruct((tokens, channels), BF16),
         jax.ShapeDtypeStruct((3, tokens, channels), BF16),
@@ -308,13 +367,14 @@
         out_specs=(in_vmem,) * 3,
         scratch_shapes=[pltpu.VMEM(operand.shape, operand.dtype) for operand in operands]
         + [
-            buffer, buffer, buffer, buffer,
+            buffer, buffer, buffer, buffer, scales, scales,
+            pltpu.VMEM((tokens, channels), F32), whole, whole,
             pltpu.VMEM((3, tokens, channels), F32),
             pltpu.VMEM((3, 16, channels), BF16),
             pltpu.VMEM((3, SUB // 2, 2 * SIDE, 2 * SIDE), F32),
             pltpu.SemaphoreType.DMA((len(operands),)),
-            pltpu.SemaphoreType.DMA((6, DEVICES)),
-            pltpu.SemaphoreType.DMA((6, DEVICES)),
+            pltpu.SemaphoreType.DMA((12, DEVICES)),
+            pltpu.SemaphoreType.DMA((12, DEVICES)),
             pltpu.SemaphoreType.DMA((2,)),
         ],
         compiler_params=pltpu.CompilerParams(

time: 50.6 us -> 44.9 us (0.89)
  Pallas kernels: 49.9 us -> 44.2 us
    pallas_call x1, Pallas kernels: 48.7 us -> 43 us  [local(): pl.pallas_call(kernel, out_shape=out_shape, in_specs=[in_hbm] * len(opera...]
where the time goes in v3:
time: 44.9 us; the launch traced here: 44.8 us
  Pallas kernels  44.2 us (98%)
  between operations  0.64 us (1%)
    pallas_call x1, Pallas kernels, local(): pl.pallas_call(kernel, out_shape=out_shape, in_specs=[in_hbm] * len(opera...  43 us
    pallas_call x1, Pallas kernels, local(): pl.pallas_call(write_out, out_shape=out_shape, in_specs=[in_vmem] * 3, ou...  1.16 us

profile of v3, /device:TPU:0, one launch (start us, length us, event | category | flops | bytes accessed | tf_op | source)
XLA Modules:
  0.0 44.8 jit_solution(15276430507943049154)
XLA Ops:
  0.6 43.0 %shard_map.112 = (bf16[1024,128]{1,0:T(8,128)(2,1)S(1)}, bf16[3,1024,128]{2,1,0:T(8,128)(2,1)S(1)}, f32[1024,128]{1,0:T(8,128)S(1)}) custom-call(f32[1024,128]{1,0:T(8,128)} %filt_hbm.1, bf16[3,1024,128]{2,1,0:T(8,128)(2,1)} %proj_hbm.1, f32[3,3,128]{2,1,0:T(4,128)} %taps_hbm.1, bf16[1024,128]{1,0:T(8,128)(2,1)} %grad_hbm.1, ...), custom_call_target="tpu_custom_call" | custom-call | tf_op jit(solution)/shard_map/pallas_call | solution.py:363
  43.6 1.2 %shard_map.113 = (bf16[1024,128]{1,0:T(8,128)(2,1)}, bf16[3,1024,128]{2,1,0:T(8,128)(2,1)}, f32[1024,128]{1,0:T(8,128)}) custom-call(bf16[1024,128]{1,0:T(8,128)(2,1)S(1)} %get-tuple-element.6.mixed, bf16[3,1024,128]{2,1,0:T(8,128)(2,1)S(1)} %get-tuple-element.7.grad_streams, f32[1024,128]{1,0:T(8,128)S(1)} %get-tuple-element.8.grad_filter), custom_call_target="tpu_custom_call" | custom-call | tf_op jit(solution)/shard_map/pallas_call | solution.py:384

commit v4 on v3

--- a/solution.py
+++ b/solution.py
@@ -99,11 +99,11 @@
     def peer_of(step):
         return (row + step // 4) % 4 * 4 + (column + step % 4) % 4
 
+    peers = [peer_of(step) for step in range(1, DEVICES)]
+
     def each_peer(action):
-        def body(step, carry):
-            action(peer_of(step))
-            return carry
-        lax.fori_loop(1, DEVICES, body, 0)
+        for peer in peers:
+            action(peer)
 
     pairs = [(sent.at[m], got.at[m]) for m in range(3)] + [(made.at[m], home.at[m]) for m in range(3)]
     pairs += [(scales_out.at[m], scales_in.at[m]) for m in range(6)]
@@ -112,16 +112,17 @@
         source, target = pairs[message]
         return pltpu.make_async_remote_copy(
             src_ref=source.at[peer], dst_ref=target.at[me],
-            send_sem=send_sem.at[message, peer], recv_sem=recv_sem.at[message, me],
+            send_sem=send_sem.at[message], recv_sem=recv_sem.at[message],
             device_id={"ctx": peer}, device_id_type=MESH,
         )
 
-    def copy_from(message, peer):
+    def all_copies(message):
         source, target = pairs[message]
+        every = pl.ds(0, DEVICES - 1)
         return pltpu.make_async_remote_copy(
-            src_ref=source.at[peer], dst_ref=target.at[peer],
-            send_sem=send_sem.at[message, peer], recv_sem=recv_sem.at[message, peer],
-            device_id={"ctx": peer}, device_id_type=MESH,
+            src_ref=source.at[every], dst_ref=target.at[every],
+            send_sem=send_sem.at[message], recv_sem=recv_sem.at[message],
+            device_id={"ctx": peers[0]}, device_id_type=MESH,
         )
 
     def send(message):
@@ -133,10 +134,8 @@
             target[me] = source[me]
 
     def receive(message):
-        def wait(peer):
-            copy_from(message + 6, peer).wait_recv()
-            copy_from(message, peer).wait_recv()
-        each_peer(wait)
+        all_copies(message + 6).wait_recv()
+        all_copies(message).wait_recv()
 
     def rows_of(block):
         return pl.ds(pl.multiple_of(block * SIDE, SIDE), SIDE)
@@ -329,7 +328,7 @@
     turned_home(4, stream_home)
     turned_home(5, filt_home)
     for message in range(12):
-        each_peer(lambda peer: copy_to(message, peer).wait_send())
+        all_copies(message).wait_send()
     halo_copy(after).wait_send()
 
 
@@ -373,8 +372,8 @@
             pltpu.VMEM((3, 16, channels), BF16),
             pltpu.VMEM((3, SUB // 2, 2 * SIDE, 2 * SIDE), F32),
             pltpu.SemaphoreType.DMA((len(operands),)),
-            pltpu.SemaphoreType.DMA((12, DEVICES)),
-            pltpu.SemaphoreType.DMA((12, DEVICES)),
+            pltpu.SemaphoreType.DMA((12,)),
+            pltpu.SemaphoreType.DMA((12,)),
             pltpu.SemaphoreType.DMA((2,)),
         ],
         compiler_params=pltpu.CompilerParams(

time: 44.9 us -> 37.1 us (0.83)
  Pallas kernels: 44.2 us -> 36.4 us
    pallas_call x1, Pallas kernels: 43 us -> 35.2 us  [local(): pl.pallas_call(kernel, out_shape=out_shape, in_specs=[in_hbm] * len(opera...]
where the time goes in v4:
time: 37.1 us; the launch traced here: 37 us
  Pallas kernels  36.4 us (98%)
  between operations  0.64 us (2%)
    pallas_call x1, Pallas kernels, local(): pl.pallas_call(kernel, out_shape=out_shape, in_specs=[in_hbm] * len(opera...  35.2 us
    pallas_call x1, Pallas kernels, local(): pl.pallas_call(write_out, out_shape=out_shape, in_specs=[in_vmem] * 3, ou...  1.16 us

profile of v4, /device:TPU:0, one launch (start us, length us, event | category | flops | bytes accessed | tf_op | source)
XLA Modules:
  0.0 37.0 jit_solution(6047067518855779909)
XLA Ops:
  0.6 35.2 %shard_map.112 = (bf16[1024,128]{1,0:T(8,128)(2,1)S(1)}, bf16[3,1024,128]{2,1,0:T(8,128)(2,1)S(1)}, f32[1024,128]{1,0:T(8,128)S(1)}) custom-call(f32[1024,128]{1,0:T(8,128)} %filt_hbm.1, bf16[3,1024,128]{2,1,0:T(8,128)(2,1)} %proj_hbm.1, f32[3,3,128]{2,1,0:T(4,128)} %taps_hbm.1, bf16[1024,128]{1,0:T(8,128)(2,1)} %grad_hbm.1, ...), custom_call_target="tpu_custom_call" | custom-call | tf_op jit(solution)/shard_map/pallas_call | solution.py:362
  35.8 1.2 %shard_map.113 = (bf16[1024,128]{1,0:T(8,128)(2,1)}, bf16[3,1024,128]{2,1,0:T(8,128)(2,1)}, f32[1024,128]{1,0:T(8,128)}) custom-call(bf16[1024,128]{1,0:T(8,128)(2,1)S(1)} %get-tuple-element.6.mixed, bf16[3,1024,128]{2,1,0:T(8,128)(2,1)S(1)} %get-tuple-element.7.grad_streams, f32[1024,128]{1,0:T(8,128)S(1)} %get-tuple-element.8.grad_filter), custom_call_target="tpu_custom_call" | custom-call | tf_op jit(solution)/shard_map/pallas_call | solution.py:383

commit v5 on v4

--- a/solution.py
+++ b/solution.py
@@ -269,19 +269,17 @@
         for pair in range(SUB // 2):
             action(pair)
 
-    def filter_pair(pair):
-        spectra[0, pair] = forward(pair)
+    def spectrum(signal):
+        def action(pair):
+            spectra[signal, pair] = forward(pair)
+        each_pair(action)
 
     def conv_pair(pair):
-        value = forward(pair)
-        spectra[1, pair] = value
-        (fr, fi), (vr, vi) = parts_of(spectra[0, pair]), parts_of(value)
+        (fr, fi), (vr, vi) = parts_of(spectra[0, pair]), parts_of(spectra[1, pair])
         inverse(pair, fr * vr - fi * vi, fr * vi + fi * vr)
 
     def stream_pair(pair):
-        value = forward(pair)
-        spectra[2, pair] = value
-        (fr, fi), (br, bi) = parts_of(spectra[0, pair]), parts_of(value)
+        (fr, fi), (br, bi) = parts_of(spectra[0, pair]), parts_of(spectra[2, pair])
         inverse(pair, fr * br + fi * bi, fr * bi - fi * br)
 
     def filt_pair(pair):
@@ -291,11 +289,13 @@
     for load in loads[4:]:
         load.wait()
     gather(0)
-    each_pair(filter_pair)
+    spectrum(0)
     gather(1)
+    spectrum(1)
     each_pair(conv_pair)
     scatter(3)
     gather(2)
+    spectrum(2)
     each_pair(stream_pair)
     scatter(4)
     each_pair(filt_pair)

time: 37.1 us -> 34.3 us (0.925)
  Pallas kernels: 36.4 us -> 33.6 us
    pallas_call x1, Pallas kernels: 35.2 us -> 32.4 us  [local(): pl.pallas_call(kernel, out_shape=out_shape, in_specs=[in_hbm] * len(opera...]
where the time goes in v5:
time: 34.3 us; the launch traced here: 34.2 us
  Pallas kernels  33.6 us (98%)
  between operations  0.64 us (2%)
    pallas_call x1, Pallas kernels, local(): pl.pallas_call(kernel, out_shape=out_shape, in_specs=[in_hbm] * len(opera...  32.4 us
    pallas_call x1, Pallas kernels, local(): pl.pallas_call(write_out, out_shape=out_shape, in_specs=[in_vmem] * 3, ou...  1.16 us

profile of v5, /device:TPU:0, one launch (start us, length us, event | category | flops | bytes accessed | tf_op | source)
XLA Modules:
  0.0 34.2 jit_solution(6553255008976573522)
XLA Ops:
  0.6 32.4 %shard_map.112 = (bf16[1024,128]{1,0:T(8,128)(2,1)S(1)}, bf16[3,1024,128]{2,1,0:T(8,128)(2,1)S(1)}, f32[1024,128]{1,0:T(8,128)S(1)}) custom-call(f32[1024,128]{1,0:T(8,128)} %filt_hbm.1, bf16[3,1024,128]{2,1,0:T(8,128)(2,1)} %proj_hbm.1, f32[3,3,128]{2,1,0:T(4,128)} %taps_hbm.1, bf16[1024,128]{1,0:T(8,128)(2,1)} %grad_hbm.1, ...), custom_call_target="tpu_custom_call" | custom-call | tf_op jit(solution)/shard_map/pallas_call | solution.py:362
  33.1 1.2 %shard_map.113 = (bf16[1024,128]{1,0:T(8,128)(2,1)}, bf16[3,1024,128]{2,1,0:T(8,128)(2,1)}, f32[1024,128]{1,0:T(8,128)}) custom-call(bf16[1024,128]{1,0:T(8,128)(2,1)S(1)} %get-tuple-element.6.mixed, bf16[3,1024,128]{2,1,0:T(8,128)(2,1)S(1)} %get-tuple-element.7.grad_streams, f32[1024,128]{1,0:T(8,128)S(1)} %get-tuple-element.8.grad_filter), custom_call_target="tpu_custom_call" | custom-call | tf_op jit(solution)/shard_map/pallas_call | solution.py:383

commit v6 on v5

--- a/solution.py
+++ b/solution.py
@@ -22,6 +22,11 @@
     high = table.astype(ml_dtypes.bfloat16)
     low = (table - high.astype(np.float64)).astype(ml_dtypes.bfloat16)
     return high, low
+
+
+def along(table, axis):
+    high, low = halves(table)
+    return np.concatenate([high, high, low], axis=axis)
 
 
 def tables():
@@ -35,7 +40,7 @@
     back = np.block([[cos, sin], [-sin, cos]])
     last = np.concatenate([np.cos(outer).T, -np.sin(outer).T], axis=1) / (SIDE * SIDE)
     twist = np.stack([np.cos(turn), np.sin(turn)]).astype(np.float32)
-    return np.stack(halves(first)), np.stack(halves(second)), np.stack(halves(back)), np.stack(halves(last)), twist
+    return along(first, 1), along(second, 0), along(back, 0), along(last, 1), twist
 
 
 def split(value):
@@ -49,12 +54,12 @@
 
 def left_product(table, value):
     high, low = split(value)
-    return dot(table[0], high) + dot(table[0], low) + dot(table[1], high)
+    return dot(table[...], jnp.concatenate([high, low, high], axis=0))
 
 
 def right_product(value, table):
     high, low = split(value)
-    return dot(high, table[0]) + dot(low, table[0]) + dot(high, table[1])
+    return dot(jnp.concatenate([high, low, high], axis=1), table[...])
 
 
 def scale_of(largest):
@@ -99,7 +104,10 @@
     def peer_of(step):
         return (row + step // 4) % 4 * 4 + (column + step % 4) % 4
 
-    peers = [peer_of(step) for step in range(1, DEVICES)]
+    def hops(step):
+        return min(step // 4, 4 - step // 4) + min(step % 4, 4 - step % 4)
+
+    peers = [peer_of(step) for step in sorted(range(1, DEVICES), key=hops, reverse=True)]
 
     def each_peer(action):
         for peer in peers:

time: 34.3 us -> 32.9 us (0.959)
  Pallas kernels: 33.6 us -> 32.2 us
    pallas_call x1, Pallas kernels: 32.4 us -> 31 us  [local(): pl.pallas_call(kernel, out_shape=out_shape, in_specs=[in_hbm] * len(opera...]
where the time goes in v6:
time: 32.9 us; the launch traced here: 32.8 us
  Pallas kernels  32.2 us (98%)
  between operations  0.64 us (2%)
    pallas_call x1, Pallas kernels, local(): pl.pallas_call(kernel, out_shape=out_shape, in_specs=[in_hbm] * len(opera...  31 us
    pallas_call x1, Pallas kernels, local(): pl.pallas_call(write_out, out_shape=out_shape, in_specs=[in_vmem] * 3, ou...  1.16 us

profile of v6, /device:TPU:0, one launch (start us, length us, event | category | flops | bytes accessed | tf_op | source)
XLA Modules:
  0.0 32.8 jit_solution(2383595649343663081)
XLA Ops:
  0.6 31.0 %shard_map.112 = (bf16[1024,128]{1,0:T(8,128)(2,1)S(1)}, bf16[3,1024,128]{2,1,0:T(8,128)(2,1)S(1)}, f32[1024,128]{1,0:T(8,128)S(1)}) custom-call(f32[1024,128]{1,0:T(8,128)} %filt_hbm.1, bf16[3,1024,128]{2,1,0:T(8,128)(2,1)} %proj_hbm.1, f32[3,3,128]{2,1,0:T(4,128)} %taps_hbm.1, bf16[1024,128]{1,0:T(8,128)(2,1)} %grad_hbm.1, ...), custom_call_target="tpu_custom_call" | custom-call | tf_op jit(solution)/shard_map/pallas_call | solution.py:370
  31.6 1.2 %shard_map.113 = (bf16[1024,128]{1,0:T(8,128)(2,1)}, bf16[3,1024,128]{2,1,0:T(8,128)(2,1)}, f32[1024,128]{1,0:T(8,128)}) custom-call(bf16[1024,128]{1,0:T(8,128)(2,1)S(1)} %get-tuple-element.6.mixed, bf16[3,1024,128]{2,1,0:T(8,128)(2,1)S(1)} %get-tuple-element.7.grad_streams, f32[1024,128]{1,0:T(8,128)S(1)} %get-tuple-element.8.grad_filter), custom_call_target="tpu_custom_call" | custom-call | tf_op jit(solution)/shard_map/pallas_call | solution.py:391

commit v7 on v6

--- a/solution.py
+++ b/solution.py
@@ -13,6 +13,7 @@
 SIDE = 128
 DEVICES = 16
 SUB = 8
+GROUP = 4
 BLOCKS = 8
 OFFSET = 1.0 / 64.0
 F32, BF16 = jnp.float32, jnp.bfloat16
@@ -246,11 +247,11 @@
         send(message)
 
     def forward(pair):
-        parts = [gathered[:, pl.ds(2 * pair + i, SUB, stride=SUB), :].reshape(SIDE, SIDE) for i in range(2)]
+        parts = [gathered[:, pl.ds(GROUP * pair + i, SUB, stride=SUB), :].reshape(SIDE, SIDE) for i in range(GROUP)]
         mixed_rows = left_product(first, jnp.concatenate(parts, axis=1))
         cos, sin = twist[0], twist[1]
         rows = []
-        for i in range(2):
+        for i in range(GROUP):
             real = mixed_rows[:SIDE, i * SIDE : (i + 1) * SIDE]
             imag = mixed_rows[SIDE:, i * SIDE : (i + 1) * SIDE]
             rows.append(jnp.concatenate([real * cos + imag * sin, imag * cos - real * sin], axis=1))
@@ -260,13 +261,13 @@
         value = right_product(jnp.concatenate([real, imag], axis=1), back)
         cos, sin = twist[0], twist[1]
         columns = []
-        for i in range(2):
+        for i in range(GROUP):
             real = value[i * SIDE : (i + 1) * SIDE, :SIDE]
             imag = value[i * SIDE : (i + 1) * SIDE, SIDE:]
             columns.append(jnp.concatenate([real * cos - imag * sin, real * sin + imag * cos], axis=0))
         result = left_product(last, jnp.concatenate(columns, axis=1))
-        for i in range(2):
-            results[:, pl.ds(2 * pair + i, SUB, stride=SUB), :] = result[:, i * SIDE : (i + 1) * SIDE].reshape(
+        for i in range(GROUP):
+            results[:, pl.ds(GROUP * pair + i, SUB, stride=SUB), :] = result[:, i * SIDE : (i + 1) * SIDE].reshape(
                 DEVICES, SUB, SIDE
             )
 
@@ -274,7 +275,7 @@
         return value[:, :SIDE], value[:, SIDE:]
 
     def each_pair(action):
-        for pair in range(SUB // 2):
+        for pair in range(SUB // GROUP):
             action(pair)
 
     def spectrum(signal):
@@ -378,7 +379,7 @@
             pltpu.VMEM((tokens, channels), F32), whole, whole,
             pltpu.VMEM((3, tokens, channels), F32),
             pltpu.VMEM((3, 16, channels), BF16),
-            pltpu.VMEM((3, SUB // 2, 2 * SIDE, 2 * SIDE), F32),
+            pltpu.VMEM((3, SUB // GROUP, GROUP * SIDE, 2 * SIDE), F32),
             pltpu.SemaphoreType.DMA((len(operands),)),
             pltpu.SemaphoreType.DMA((12,)),
             pltpu.SemaphoreType.DMA((12,)),

time: 32.9 us -> 31.7 us (0.964)
  Pallas kernels: 32.2 us -> 31 us
    pallas_call x1, Pallas kernels: 31 us -> 29.8 us  [local(): pl.pallas_call(kernel, out_shape=out_shape, in_specs=[in_hbm] * len(opera...]
where the time goes in v7:
time: 31.7 us; the launch traced here: 31.6 us
  Pallas kernels  31 us (98%)
  between operations  0.64 us (2%)
    pallas_call x1, Pallas kernels, local(): pl.pallas_call(kernel, out_shape=out_shape, in_specs=[in_hbm] * len(opera...  29.8 us
    pallas_call x1, Pallas kernels, local(): pl.pallas_call(write_out, out_shape=out_shape, in_specs=[in_vmem] * 3, ou...  1.16 us

profile of v7, /device:TPU:0, one launch (start us, length us, event | category | flops | bytes accessed | tf_op | source)
XLA Modules:
  0.0 31.6 jit_solution(9333678514310180377)
XLA Ops:
  0.6 29.8 %shard_map.112 = (bf16[1024,128]{1,0:T(8,128)(2,1)S(1)}, bf16[3,1024,128]{2,1,0:T(8,128)(2,1)S(1)}, f32[1024,128]{1,0:T(8,128)S(1)}) custom-call(f32[1024,128]{1,0:T(8,128)} %filt_hbm.1, bf16[3,1024,128]{2,1,0:T(8,128)(2,1)} %proj_hbm.1, f32[3,3,128]{2,1,0:T(4,128)} %taps_hbm.1, bf16[1024,128]{1,0:T(8,128)(2,1)} %grad_hbm.1, ...), custom_call_target="tpu_custom_call" | custom-call | tf_op jit(solution)/shard_map/pallas_call | solution.py:371
  30.4 1.2 %shard_map.113 = (bf16[1024,128]{1,0:T(8,128)(2,1)}, bf16[3,1024,128]{2,1,0:T(8,128)(2,1)}, f32[1024,128]{1,0:T(8,128)}) custom-call(bf16[1024,128]{1,0:T(8,128)(2,1)S(1)} %get-tuple-element.6.mixed, bf16[3,1024,128]{2,1,0:T(8,128)(2,1)S(1)} %get-tuple-element.7.grad_streams, f32[1024,128]{1,0:T(8,128)S(1)} %get-tuple-element.8.grad_filter), custom_call_target="tpu_custom_call" | custom-call | tf_op jit(solution)/shard_map/pallas_call | solution.py:392

commit v8 on v7

--- a/solution.py
+++ b/solution.py
@@ -87,7 +87,7 @@
     filt_hbm, proj_hbm, taps_hbm, grad_hbm, first_hbm, second_hbm, twist_hbm, back_hbm, last_hbm,
     mixed, grad_streams, grad_filter,
     filt, proj, taps, grad, first, second, twist, back, last,
-    sent, got, made, home, scales_out, scales_in, plain, gathered, results, streams, halo, spectra,
+    sent, got, made, home, scales_out, scales_in, plain, plain_back, gathered, results, streams, halo, spectra,
     load_sem, send_sem, recv_sem, halo_sem,
 ):
     loads = [
@@ -204,7 +204,7 @@
         plain[rows_of(block), :] = short(1, block, previous(1)) * short(2, block, previous(2))
 
     def back_gated(block, previous):
-        plain[rows_of(block), :] = short(0, block, previous(0)) * grad[rows_of(block), :].astype(F32)
+        plain_back[rows_of(block), :] = short(0, block, previous(0)) * grad[rows_of(block), :].astype(F32)
 
     def later_blocks(make):
         def body(block, carry):
@@ -214,14 +214,14 @@
 
     loads[2].wait()
     later_blocks(key_value)
+    loads[3].wait()
+    later_blocks(back_gated)
     halo_copy(before).wait_recv()
     key_value(0, edge)
     turned_out(1, plain)
     send(1)
-    loads[3].wait()
-    later_blocks(back_gated)
     back_gated(0, edge)
-    turned_out(2, plain)
+    turned_out(2, plain_back)
     send(2)
 
     def lane_is_own(shape, axis):
@@ -335,10 +335,12 @@
 
     turned_home(3, conv_home)
     turned_home(4, stream_home)
-    turned_home(5, filt_home)
-    for message in range(12):
+    for message in (0, 1, 2, 3, 4, 6, 7, 8, 9, 10):
         all_copies(message).wait_send()
     halo_copy(after).wait_send()
+    turned_home(5, filt_home)
+    for message in (5, 11):
+        all_copies(message).wait_send()
 
 
 def write_out(mixed, grad_streams, grad_filter, mixed_hbm, grad_streams_hbm, grad_filter_hbm, sems):
@@ -376,7 +378,7 @@
         scratch_shapes=[pltpu.VMEM(operand.shape, operand.dtype) for operand in operands]
         + [
             buffer, buffer, buffer, buffer, scales, scales,
-            pltpu.VMEM((tokens, channels), F32), whole, whole,
+            pltpu.VMEM((tokens, channels), F32), pltpu.VMEM((tokens, channels), F32), whole, whole,
             pltpu.VMEM((3, tokens, channels), F32),
             pltpu.VMEM((3, 16, channels), BF16),
             pltpu.VMEM((3, SUB // GROUP, GROUP * SIDE, 2 * SIDE), F32),

time: 31.7 us -> 31.7 us (level)
  no operation moved by 1% of the time
where the time goes in v8:
time: 31.7 us; the launch traced here: 31.6 us
  Pallas kernels  31 us (98%)
  between operations  0.64 us (2%)
    pallas_call x1, Pallas kernels, local(): pl.pallas_call(kernel, out_shape=out_shape, in_specs=[in_hbm] * len(opera...  29.8 us
    pallas_call x1, Pallas kernels, local(): pl.pallas_call(write_out, out_shape=out_shape, in_specs=[in_vmem] * 3, ou...  1.16 us

profile of v8, /device:TPU:0, one launch (start us, length us, event | category | flops | bytes accessed | tf_op | source)
XLA Modules:
  0.0 31.6 jit_solution(10830571797478065603)
XLA Ops:
  0.6 29.8 %shard_map.112 = (bf16[1024,128]{1,0:T(8,128)(2,1)S(1)}, bf16[3,1024,128]{2,1,0:T(8,128)(2,1)S(1)}, f32[1024,128]{1,0:T(8,128)S(1)}) custom-call(f32[1024,128]{1,0:T(8,128)} %filt_hbm.1, bf16[3,1024,128]{2,1,0:T(8,128)(2,1)} %proj_hbm.1, f32[3,3,128]{2,1,0:T(4,128)} %taps_hbm.1, bf16[1024,128]{1,0:T(8,128)(2,1)} %grad_hbm.1, ...), custom_call_target="tpu_custom_call" | custom-call | tf_op jit(solution)/shard_map/pallas_call | solution.py:373
  30.4 1.2 %shard_map.113 = (bf16[1024,128]{1,0:T(8,128)(2,1)}, bf16[3,1024,128]{2,1,0:T(8,128)(2,1)}, f32[1024,128]{1,0:T(8,128)}) custom-call(bf16[1024,128]{1,0:T(8,128)(2,1)S(1)} %get-tuple-element.6.mixed, bf16[3,1024,128]{2,1,0:T(8,128)(2,1)S(1)} %get-tuple-element.7.grad_streams, f32[1024,128]{1,0:T(8,128)S(1)} %get-tuple-element.8.grad_filter), custom_call_target="tpu_custom_call" | custom-call | tf_op jit(solution)/shard_map/pallas_call | solution.py:394
